TPU v7x, 128 devices: a whole 4x4x4 slice. The times are simulated.
128 devices in a mesh: dp: 64 (over z_lo, x, y, core), tensor: 2 (over z_hi).
Axes of the slice: x: 4, y: 4, z: 4 (z_hi: 2, z_lo: 2; z = z_hi * 2 + z_lo), core: 2. Of those that a mesh axis runs over, the one named last changes fastest.
Arguments:
- tokens: bfloat16 [16384, 1152], P(('dp', 'tensor')), may hold values from -6 to 6
- segment_ids: int32 [64, 256], P('dp'), may hold values from 0 to 7, never falling along the last dimension, each value on 1 to 192 neighbouring positions
- w_query: bfloat16 [1152, 1024], P('dp', 'tensor'), may hold values from -1 to 1
- w_key: bfloat16 [1152, 256], P('dp'), may hold values from -1 to 1
- w_value: bfloat16 [1152, 256], P('dp'), may hold values from -0.1875 to 0.1875
- w_out: bfloat16 [1152, 1024], P('dp', 'tensor'), may hold values from -0.1875 to 0.1875
- gain_query: bfloat16 [256], P('dp'), may hold values from -1 to 4
- gain_key: bfloat16 [256], P('dp'), may hold values from -1 to 4
- gain_pre_attn: bfloat16 [1152], P('dp'), may hold values from -0.5 to 0.5
- gain_post_attn: bfloat16 [1152], P('dp'), may hold values from -0.5 to 0.5
- w_gate: bfloat16 [1152, 6912], P('dp', 'tensor'), may hold values from -0.1875 to 0.1875
- w_up: bfloat16 [1152, 6912], P('dp', 'tensor'), may hold values from -0.1875 to 0.1875
- w_down: bfloat16 [1152, 6912], P('dp', 'tensor'), may hold values from -0.078125 to 0.078125
- gain_pre_ffn: bfloat16 [1152], P('dp'), may hold values from -0.5 to 0.5
- gain_post_ffn: bfloat16 [1152], P('dp'), may hold values from -0.5 to 0.5
- cotangent: bfloat16 [16384, 1152], P(('dp', 'tensor')), may hold values from -6 to 6
Outputs:
- output: bfloat16 [16384, 1152], P(('dp', 'tensor'))
- grad_tokens: float32 [16384, 1152], P(('dp', 'tensor'))
- grad_w_query: float32 [1152, 1024], P('dp', 'tensor')
- grad_w_key: float32 [1152, 256], P('dp')
- grad_w_value: float32 [1152, 256], P('dp')
- grad_w_out: float32 [1152, 1024], P('dp', 'tensor')
- grad_gain_query: float32 [256], P('dp')
- grad_gain_key: float32 [256], P('dp')
- grad_gain_pre_attn: float32 [1152], P('dp')
- grad_gain_post_attn: float32 [1152], P('dp')
- grad_w_gate: float32 [1152, 6912], P('dp', 'tensor')
- grad_w_up: float32 [1152, 6912], P('dp', 'tensor')
- grad_w_down: float32 [1152, 6912], P('dp', 'tensor')
- grad_gain_pre_ffn: float32 [1152], P('dp')
- grad_gain_post_ffn: float32 [1152], P('dp')
Inputs may be any that keep to these rules, and one draw needn't show every extreme that they name: `segment_ids`: in each pack the ids run from 0 to 7 without falling; every sequence has 1 to 192 tokens and one has exactly 192.
All inputs are finite; a program needn't handle non-finite values.
Results may differ from a plain program's by a relative error of at most 0.024.
The roundings to bfloat16 on the way count: a program that leaves them out, or rounds other values in their place, can miss the bound.
Values may be sent and summed in bfloat16 or wider, within the bound.
A program may use at most 192 MiB of HBM per device.

v0:
```python
import math

import jax
import jax.numpy as jnp
from jax import lax
from jax.sharding import PartitionSpec as P

eps = 1e-06
gelu_scale = 0.7978845608028654
gelu_cube = 0.044715


def in_one_piece(arrays, axis, dim, along):
    ends, at = ([], 0)
    for a in arrays[:-1]:
        at += a.shape[along]
        ends.append(at)
    both = jnp.concatenate(arrays, axis=along)
    return tuple(jnp.split(lax.all_gather(both, axis, axis=dim, tiled=True), ends, axis=along))


def copy_for_each(value, axis):
    copies = jnp.broadcast_to(value, (lax.axis_size(axis), *value.shape))
    return lax.all_to_all(copies, axis, split_axis=0, concat_axis=0, tiled=True)


def in_order(pieces, dim):
    pieces = jnp.moveaxis(pieces, 0, dim)
    shape = pieces.shape
    return pieces.reshape(*shape[:dim], shape[dim] * shape[dim + 1], *shape[dim + 2 :])


def gather_directly(value, axis, dim):
    pieces = copy_for_each(value, axis)
    return in_order(pieces, dim)


def split_up(value, dim, count):
    before, after = (value.shape[:dim], value.shape[dim + 1 :])
    return jnp.moveaxis(value.reshape(*before, count, -1, *after), dim, 0)


def sent_and_summed(value, axis, dim):
    count = lax.axis_size(axis)
    pieces = lax.all_to_all(split_up(value, dim, count), axis, 0, 0, tiled=True)
    return jnp.sum(pieces, axis=0)


def sent_together(arrays, axis, dim, along):
    widths = [math.prod(a.shape[along:]) for a in arrays]
    both = jnp.concatenate(
        [a.reshape(*a.shape[:along], w) for a, w in zip(arrays, widths)], axis=along
    )
    result = lax.all_gather(both, axis, axis=dim, tiled=True)
    pieces = jnp.split(result, [sum(widths[:k]) for k in range(1, len(widths))], axis=along)
    return tuple(
        (b.reshape(*result.shape[:along], *a.shape[along:]) for a, b in zip(arrays, pieces))
    )


def sum_at_owner(value, axis, dim):
    count = lax.axis_size(axis)
    pieces = lax.all_to_all(split_up(value, dim, count), axis, 0, 0, tiled=True)
    return jnp.sum(pieces.astype(jnp.float32), axis=0)


def over_copies(value, axis):
    everything = copy_for_each(value, axis)
    return jnp.sum(everything.astype(jnp.float32), axis=0)


def rms_apply(values, gain_vec):
    inverse = lax.rsqrt(jnp.mean(values * values, axis=-1, keepdims=True) + eps)
    return (values * inverse * (1.0 + gain_vec), inverse)


def rms_back(values, inverse, gain_vec, grad_out):
    scaled = grad_out * (1.0 + gain_vec)
    grad_value = inverse * scaled - values * inverse * inverse * inverse * jnp.mean(
        scaled * values, axis=-1, keepdims=True
    )
    grad_gain = jnp.sum(grad_out * values * inverse, axis=tuple(range(values.ndim - 1)))
    return (grad_value, grad_gain)


def gelu_pair(values):
    tanh_value = jnp.tanh(gelu_scale * (values + gelu_cube * values * values * values))
    result = 0.5 * values * (1.0 + tanh_value)
    slope = 0.5 * (1.0 + tanh_value) + 0.5 * values * (
        1.0 - tanh_value * tanh_value
    ) * gelu_scale * (1.0 + 3.0 * gelu_cube * values * values)
    return (result, slope)


def positions_of(segment_row):
    token_index = jnp.arange(segment_row.shape[0], dtype=jnp.int32)
    earlier = jnp.concatenate([segment_row[:1] - 1, segment_row[:-1]])
    starts = lax.cummax(jnp.where(segment_row != earlier, token_index, 0), axis=0)
    return token_index - starts


def build_allowed(segment_row):
    token_index = jnp.arange(segment_row.shape[0], dtype=jnp.int32)
    same_seq = segment_row[:, None] == segment_row[None, :]
    causal = token_index[None, :] <= token_index[:, None]
    return same_seq & causal


def rope_tables(position, width):
    half_width = width // 2
    frequency = jnp.exp(
        jnp.arange(half_width, dtype=jnp.float32) * (-2.0 * math.log(10000.0) / width)
    )
    angles = position.astype(jnp.float32)[:, None] * frequency[None, :]
    cosine_table = jnp.concatenate([jnp.cos(angles), jnp.cos(angles)], axis=1)
    sine_table = jnp.concatenate([jnp.sin(angles), jnp.sin(angles)], axis=1)
    return (cosine_table, sine_table)


def rotate_half(values):
    half_width = values.shape[-1] // 2
    return jnp.concatenate([-values[..., half_width:], values[..., :half_width]], axis=-1)


def split_rows(member, count):
    return member.reshape((count, member.shape[0] // count) + member.shape[1:])


def add_sources(received):
    return tuple((jnp.sum(member, axis=0) for member in received))


def local(
    tokens,
    segment_ids,
    w_query,
    w_key,
    w_value,
    w_out,
    gain_query,
    gain_key,
    gain_pre_attn,
    gain_post_attn,
    w_gate,
    w_up,
    w_down,
    gain_pre_ffn,
    gain_post_ffn,
    cotangent,
):
    f32 = jnp.float32
    bf16 = jnp.bfloat16
    shard_count = lax.axis_size("dp")
    attn_set = (
        *in_one_piece((w_query, w_key, w_value, w_out), "dp", 0, 1),
        lax.all_gather(gain_query, "dp", axis=0, tiled=True),
        lax.all_gather(gain_key, "dp", axis=0, tiled=True),
        lax.all_gather(gain_pre_attn, "dp", axis=0, tiled=True),
        lax.all_gather(gain_post_attn, "dp", axis=0, tiled=True),
    )
    query_mat, key_mat, value_mat, out_mat = (attn_set[0], attn_set[1], attn_set[2], attn_set[3])
    gain_q = attn_set[4].astype(f32)
    gain_k = attn_set[5].astype(f32)
    gain_pa = attn_set[6].astype(f32)
    gain_po = attn_set[7].astype(f32)
    head_size = key_mat.shape[1]
    heads_local = query_mat.shape[1] // head_size
    resid_in = tokens.astype(f32)
    attn_local, r_one = rms_apply(resid_in, gain_pa)
    attn_in = gather_directly(attn_local.astype(bf16), "tensor", 0)
    row_count = attn_in.shape[0]
    segment_row = segment_ids[0]
    position = positions_of(segment_row)
    allowed = build_allowed(segment_row)
    query_raw = jnp.dot(attn_in, query_mat, preferred_element_type=f32).reshape(
        row_count, heads_local, head_size
    )
    key_raw = jnp.dot(attn_in, key_mat, preferred_element_type=f32)
    value_vec = jnp.dot(attn_in, value_mat, preferred_element_type=f32).astype(bf16)
    query_norm, r_query = rms_apply(query_raw, gain_q)
    key_norm, r_key = rms_apply(key_raw, gain_k)
    cosine_table, sine_table = rope_tables(position, head_size)
    query_rot = (
        query_norm * cosine_table[:, None, :] + rotate_half(query_norm) * sine_table[:, None, :]
    ).astype(bf16)
    key_rot = (key_norm * cosine_table + rotate_half(key_norm) * sine_table).astype(bf16)
    score_scale = head_size ** (-0.5)
    scores = jnp.einsum("qhd,kd->hqk", query_rot, key_rot, preferred_element_type=f32) * score_scale
    scores = jnp.where(allowed[None], scores, -jnp.inf)
    row_max = jnp.max(scores, axis=-1, keepdims=True)
    row_total = jnp.sum(jnp.exp(scores - row_max), axis=-1, keepdims=True)
    log_total = row_max + jnp.log(row_total)
    weights_full = jnp.where(allowed[None], jnp.exp(scores - log_total), 0.0)
    probs = weights_full.astype(bf16)
    context = (
        jnp.einsum("hqk,kd->qhd", probs, value_vec, preferred_element_type=f32)
        .astype(bf16)
        .reshape(row_count, heads_local * head_size)
    )
    attn_part = jnp.einsum("te,de->td", context, out_mat, preferred_element_type=f32)
    attn_raw = sent_and_summed(attn_part, "tensor", 0)
    attn_normed, r_two = rms_apply(attn_raw, gain_po)
    residual = resid_in + attn_normed
    ffn_set = sent_together((w_gate, w_up, w_down, gain_pre_ffn, gain_post_ffn), "dp", 0, 1)
    gate_mat, up_mat, down_mat = (ffn_set[0], ffn_set[1], ffn_set[2])
    gain_pf = ffn_set[3].astype(f32)
    gain_pp = ffn_set[4].astype(f32)
    ffn_local, r_three = rms_apply(residual, gain_pf)
    ffn_input = gather_directly(ffn_local.astype(bf16), "tensor", 0)
    gate_pre = jnp.dot(ffn_input, gate_mat, preferred_element_type=f32)
    up_proj = jnp.dot(ffn_input, up_mat, preferred_element_type=f32)
    gate_act, gate_slope = gelu_pair(gate_pre)
    hidden_act = (gate_act * up_proj).astype(bf16)
    ffn_part = jnp.einsum("tf,df->td", hidden_act, down_mat, preferred_element_type=f32)
    ffn_raw = sent_and_summed(ffn_part, "tensor", 0)
    ffn_normed, r_four = rms_apply(ffn_raw, gain_pp)
    output = (residual + ffn_normed).astype(bf16)
    grad_out = cotangent.astype(f32)
    d_ffn_local, grad_gpp = rms_back(ffn_raw, r_four, gain_pp, grad_out)
    d_ffn_raw = gather_directly(d_ffn_local.astype(bf16), "tensor", 0)
    d_hidden = jnp.dot(d_ffn_raw, down_mat, preferred_element_type=f32)
    grad_down = jnp.einsum("td,tf->df", d_ffn_raw, hidden_act, preferred_element_type=f32)
    d_gate = (d_hidden * up_proj * gate_slope).astype(bf16)
    d_up = (d_hidden * gate_act).astype(bf16)
    d_input_part = jnp.einsum(
        "tf,df->td", d_gate, gate_mat, preferred_element_type=f32
    ) + jnp.einsum("tf,df->td", d_up, up_mat, preferred_element_type=f32)
    d_ffn_input = sent_and_summed(d_input_part, "tensor", 0)
    grad_gate = jnp.einsum("td,tf->df", ffn_input, d_gate, preferred_element_type=f32)
    grad_up = jnp.einsum("td,tf->df", ffn_input, d_up, preferred_element_type=f32)
    d_resid_norm, grad_gpf = rms_back(residual, r_three, gain_pf, d_ffn_input)
    d_residual = grad_out + d_resid_norm
    d_attn_local, grad_gpo = rms_back(attn_raw, r_two, gain_po, d_residual)
    d_attn_raw = gather_directly(d_attn_local.astype(bf16), "tensor", 0)
    d_context = jnp.dot(d_attn_raw, out_mat, preferred_element_type=f32).astype(bf16)
    grad_out_mat = jnp.einsum("td,te->de", d_attn_raw, context, preferred_element_type=f32)
    d_context = d_context.reshape(row_count, heads_local, head_size)
    d_prob = jnp.einsum("qhd,kd->hqk", d_context, value_vec, preferred_element_type=f32)
    delta = jnp.sum(weights_full * d_prob, axis=-1, keepdims=True)
    d_score = (weights_full * (d_prob - delta) * score_scale).astype(bf16)
    d_query_rot = jnp.einsum("hqk,kd->qhd", d_score, key_rot, preferred_element_type=f32)
    d_query_norm = d_query_rot * cosine_table[:, None, :] - rotate_half(
        d_query_rot * sine_table[:, None, :]
    )
    d_query, grad_gq = rms_back(query_raw, r_query, gain_q, d_query_norm)
    d_query = d_query.astype(bf16).reshape(row_count, heads_local * head_size)
    d_key_rot = jnp.einsum("hqk,qhd->kd", d_score, query_rot, preferred_element_type=f32)
    d_key_norm = d_key_rot * cosine_table - rotate_half(d_key_rot * sine_table)
    d_key, grad_gk = rms_back(key_raw, r_key, gain_k, d_key_norm)
    d_key = d_key.astype(bf16)
    d_value = jnp.einsum("hqk,qhd->kd", probs, d_context, preferred_element_type=f32).astype(bf16)
    d_in_part = jnp.einsum("te,de->td", d_query, query_mat, preferred_element_type=f32)
    d_in_part = d_in_part + jnp.einsum("te,de->td", d_key, key_mat, preferred_element_type=f32)
    d_in_part = d_in_part + jnp.einsum("te,de->td", d_value, value_mat, preferred_element_type=f32)
    d_attn_in = sum_at_owner(d_in_part.astype(jnp.bfloat16), "tensor", 0)
    grad_query = jnp.einsum("td,te->de", attn_in, d_query, preferred_element_type=f32)
    grad_key = jnp.einsum("td,te->de", attn_in, d_key, preferred_element_type=f32)
    grad_value = jnp.einsum("td,te->de", attn_in, d_value, preferred_element_type=f32)
    d_input_norm, grad_gpa = rms_back(resid_in, r_one, gain_pa, d_attn_in)
    grad_tokens = d_residual + d_input_norm
    every_term = (
        grad_query,
        grad_key,
        grad_value,
        grad_out_mat,
        grad_gq,
        grad_gk,
        grad_gpa,
        grad_gpo,
        grad_gate,
        grad_up,
        grad_down,
        grad_gpf,
        grad_gpp,
    )
    every_recv = (
        lax.all_to_all(
            split_rows(every_term[0], shard_count).astype(jnp.bfloat16),
            "dp",
            split_axis=0,
            concat_axis=0,
            tiled=True,
        ).astype(jnp.float32),
        lax.all_to_all(
            split_rows(every_term[1], shard_count).astype(jnp.bfloat16),
            "dp",
            split_axis=0,
            concat_axis=0,
            tiled=True,
        ).astype(jnp.float32),
        lax.all_to_all(
            split_rows(every_term[2], shard_count).astype(jnp.bfloat16),
            "dp",
            split_axis=0,
            concat_axis=0,
            tiled=True,
        ).astype(jnp.float32),
        lax.all_to_all(
            split_rows(every_term[3], shard_count).astype(jnp.bfloat16),
            "dp",
            split_axis=0,
            concat_axis=0,
            tiled=True,
        ).astype(jnp.float32),
        lax.all_to_all(
            split_rows(every_term[4], shard_count).astype(jnp.bfloat16),
            "dp",
            split_axis=0,
            concat_axis=0,
            tiled=True,
        ).astype(jnp.float32),
        lax.all_to_all(
            split_rows(every_term[5], shard_count).astype(jnp.bfloat16),
            "dp",
            split_axis=0,
            concat_axis=0,
            tiled=True,
        ).astype(jnp.float32),
        lax.all_to_all(
            split_rows(every_term[6], shard_count).astype(jnp.bfloat16),
            "dp",
            split_axis=0,
            concat_axis=0,
            tiled=True,
        ).astype(jnp.float32),
        lax.all_to_all(
            split_rows(every_term[7], shard_count).astype(jnp.bfloat16),
            "dp",
            split_axis=0,
            concat_axis=0,
            tiled=True,
        ).astype(jnp.float32),
        lax.all_to_all(
            split_rows(every_term[8], shard_count).astype(jnp.bfloat16),
            "dp",
            split_axis=0,
            concat_axis=0,
            tiled=True,
        ).astype(jnp.float32),
        lax.all_to_all(
            split_rows(every_term[9], shard_count).astype(jnp.bfloat16),
            "dp",
            split_axis=0,
            concat_axis=0,
            tiled=True,
        ).astype(jnp.float32),
        lax.all_to_all(
            split_rows(every_term[10], shard_count).astype(jnp.bfloat16),
            "dp",
            split_axis=0,
            concat_axis=0,
            tiled=True,
        ).astype(jnp.float32),
        lax.all_to_all(
            split_rows(every_term[11], shard_count).astype(jnp.bfloat16),
            "dp",
            split_axis=0,
            concat_axis=0,
            tiled=True,
        ).astype(jnp.float32),
        lax.all_to_all(
            split_rows(every_term[12], shard_count).astype(jnp.bfloat16),
            "dp",
            split_axis=0,
            concat_axis=0,
            tiled=True,
        ).astype(jnp.float32),
    )
    every_share = add_sources(every_recv)
    attn_shares = every_share[:8]
    ffn_shares = every_share[8:]
    shared = (
        over_copies(attn_shares[1].astype(jnp.bfloat16), "tensor").astype(jnp.float32),
        over_copies(attn_shares[2].astype(jnp.bfloat16), "tensor").astype(jnp.float32),
        over_copies(attn_shares[4].astype(jnp.bfloat16), "tensor").astype(jnp.float32),
        over_copies(attn_shares[5].astype(jnp.bfloat16), "tensor").astype(jnp.float32),
        over_copies(attn_shares[6].astype(jnp.bfloat16), "tensor").astype(jnp.float32),
        over_copies(attn_shares[7].astype(jnp.bfloat16), "tensor").astype(jnp.float32),
        over_copies(ffn_shares[3].astype(jnp.bfloat16), "tensor").astype(jnp.float32),
        over_copies(ffn_shares[4].astype(jnp.bfloat16), "tensor").astype(jnp.float32),
    )
    return (
        output,
        grad_tokens,
        attn_shares[0],
        shared[0],
        shared[1],
        attn_shares[3],
        shared[2],
        shared[3],
        shared[4],
        shared[5],
        ffn_shares[0],
        ffn_shares[1],
        ffn_shares[2],
        shared[6],
        shared[7],
    )


def solution(mesh):
    return jax.shard_map(
        local,
        mesh=mesh,
        in_specs=(
            P(("dp", "tensor"), None),
            P("dp", None),
            P("dp", "tensor"),
            P("dp", None),
            P("dp", None),
            P("dp", "tensor"),
            P("dp"),
            P("dp"),
            P("dp"),
            P("dp"),
            P("dp", "tensor"),
            P("dp", "tensor"),
            P("dp", "tensor"),
            P("dp"),
            P("dp"),
            P(("dp", "tensor"), None),
        ),
        out_specs=(
            P(("dp", "tensor"), None),
            P(("dp", "tensor"), None),
            P("dp", "tensor"),
            P("dp", None),
            P("dp", None),
            P("dp", "tensor"),
            P("dp"),
            P("dp"),
            P("dp"),
            P("dp"),
            P("dp", "tensor"),
            P("dp", "tensor"),
            P("dp", "tensor"),
            P("dp"),
            P("dp"),
        ),
        check_vma=False,
    )
```

profile of v0, /device:TPU:45, one launch (start us, length us, event | category | flops | bytes accessed | tf_op | source)
XLA Modules:
  0.0 1293.9 jit_solution(9657497111534280104)
XLA Ops:
  18.2 111.9 %all-reduce.4 = (bf16[1152]{0:T(1024)(128)(2,1)S(1)}, bf16[256]{0:T(256)(128)(2,1)S(1)}, bf16[256]{0:T(256)(128)(2,1)S(1)}, bf16[1152]{0:T(1024)(128)(2,1)}) all-reduce(bf16[1152]{0:T(1024)(128)(2,1)S(1)} %dynamic-update-slice, bf16[256]{0:T(256)(128)(2,1)S(1)} %dynamic-update-slice.1, ...), channel_id=1, replica_groups=mesh['dp'=64,'tensor'=2] {'dp'}, use_global_device_ids=true, to_apply=%add | all-reduce | flops 2816 | bytes 11264
  168.9 15.4 %all-to-all-done.1 = f32[2,128,1152]{2,1,0:T(8,128)S(1)} async-done(((f32[2,128,1152]{2,1,0:T(8,128)}), f32[2,128,1152]{2,1,0:T(8,128)S(1)}, u32[]{:S(2)}, u32[]{:S(2)}) %all-to-all-start.1) | async-done | bytes 1179680 | tf_op jit(solution)/shard_map/all_to_all | solution.py:45
  185.0 124.6 %all-gather.7.cloned.1.call-done = bf16[64,18,10370]{2,1,0:T(8,128)(2,1)} async-done(((bf16[1,18,10370]{2,1,0:T(8,128)(2,1)}), bf16[64,18,10370]{2,1,0:T(8,128)(2,1)}) %all-gather.7.cloned.1.call-update) | async-done | bytes 23892496 | tf_op jit(solution)/shard_map/all_gather | solution.py:54
  309.6 28.7 %reshape.417 = bf16[1152,10370]{1,0:T(8,128)(2,1)} reshape(bf16[64,18,10370]{2,1,0:T(8,128)(2,1)} %all-gather.7.cloned.1.call-done) | data formatting | bytes 47784960
  340.2 13.9 %all_to_all.157 = bf16[2,128,1152]{1,2,0:T(8,128)(2,1)S(1)} all-to-all(bf16[2,128,1152]{1,2,0:T(8,128)(2,1)S(1)} %broadcast_in_dim.51), channel_id=1, replica_groups=mesh['dp'=64,'tensor'=2] {'tensor'}, dimensions={0} | all-to-all | bytes 1179648 | tf_op jit(solution)/shard_map/all_to_all | solution.py:24
  354.4 7.8 fusion.11
  375.6 17.8 %all_to_all.158 = f32[2,128,1152]{2,1,0:T(8,128)S(1)} all-to-all(f32[2,128,1152]{2,1,0:T(8,128)S(1)} %bitcast.133), channel_id=1, replica_groups=mesh['dp'=64,'tensor'=2] {'tensor'}, dimensions={0} | all-to-all | bytes 2359296 | tf_op jit(solution)/shard_map/all_to_all | solution.py:45
  395.7 11.4 all_to_all.159
  409.3 7.9 fusion.19
  429.7 16.3 %all_to_all.160 = f32[2,128,1152]{2,1,0:T(8,128)S(1)} all-to-all(f32[2,128,1152]{2,1,0:T(8,128)S(1)} %bitcast.132), channel_id=1, replica_groups=mesh['dp'=64,'tensor'=2] {'tensor'}, dimensions={0} | all-to-all | bytes 2359296 | tf_op jit(solution)/shard_map/all_to_all | solution.py:45
  467.9 20.3 %all-to-all-start.27 = ((bf16[64,1,18]{2,1,0:T(2,128)(2,1)}), bf16[64,1,18]{2,1,0:T(2,128)(2,1)}, u32[]{:S(2)}, u32[]{:S(2)}) async-start(bf16[64,1,18]{2,1,0:T(2,128)(2,1)} %convert_element_type.331), calls=%async_computation.27 | async-start | bytes 65536 | tf_op jit(solution)/shard_map/all_to_all | solution.py:361
  509.7 9.1 all-to-all-start.20
  522.7 9.3 all-to-all-start.25
  549.3 9.3 all-to-all-start.14
  562.5 8.6 all-to-all-start.16
  575.1 9.0 all-to-all-start.18
  631.4 15.2 %all-to-all-start.9 = ((bf16[64,18,256]{2,1,0:T(8,128)(2,1)}), bf16[64,18,256]{2,1,0:T(8,128)(2,1)S(1)}, u32[]{:S(2)}, u32[]{:S(2)}) async-start(bf16[64,18,256]{2,1,0:T(8,128)(2,1)} %copy.281), calls=%async_computation.9 | async-start | bytes 1572864 | tf_op jit(solution)/shard_map/all_to_all | solution.py:284
  648.3 9.4 all-to-all-done.9
  657.7 8.3 all-to-all-start.11
  666.2 10.9 all-to-all-done.11
  693.9 10.6 all-to-all-start.8
  709.2 14.2 %all-to-all-done.8 = bf16[64,18,512]{2,1,0:T(8,128)(2,1)S(1)} async-done(((bf16[64,18,512]{2,1,0:T(8,128)(2,1)}), bf16[64,18,512]{2,1,0:T(8,128)(2,1)S(1)}, u32[]{:S(2)}, u32[]{:S(2)}) %all-to-all-start.8) | async-done | bytes 1179680 | tf_op jit(solution)/shard_map/all_to_all | solution.py:277
  723.4 9.8 all-to-all-start.13
  742.4 11.6 copy.305
  754.1 9.6 all-to-all-start.24
  772.9 11.7 copy.300
  784.6 145.1 %all-to-all-done.24 = bf16[64,18,3456]{2,1,0:T(8,128)(2,1)} async-done(((bf16[64,18,3456]{2,1,0:T(8,128)(2,1)}), bf16[64,18,3456]{2,1,0:T(8,128)(2,1)}, u32[]{:S(2)}, u32[]{:S(2)}) %all-to-all-start.24) | async-done | bytes 7962656 | tf_op jit(solution)/shard_map/all_to_all | solution.py:347
  929.6 9.2 all-to-all-start.22
  945.7 11.8 copy.302
  957.6 147.3 %all-to-all-done.22 = bf16[64,18,3456]{2,1,0:T(8,128)(2,1)} async-done(((bf16[64,18,3456]{2,1,0:T(8,128)(2,1)}), bf16[64,18,3456]{2,1,0:T(8,128)(2,1)}, u32[]{:S(2)}, u32[]{:S(2)}) %all-to-all-start.22) | async-done | bytes 7962656 | tf_op jit(solution)/shard_map/all_to_all | solution.py:333
  1104.9 9.2 all-to-all-start.23
  1135.8 144.3 %all-to-all-done.23 = bf16[64,18,3456]{2,1,0:T(8,128)(2,1)} async-done(((bf16[64,18,3456]{2,1,0:T(8,128)(2,1)}), bf16[64,18,3456]{2,1,0:T(8,128)(2,1)}, u32[]{:S(2)}, u32[]{:S(2)}) %all-to-all-start.23) | async-done | bytes 7962656 | tf_op jit(solution)/shard_map/all_to_all | solution.py:340
  (338 shorter events, 276.7 us)
Async XLA Ops:
  7.2 135.7 %all-gather.5.cloned.1.call-start = ((), (), s32[]{:S(2)}) async-start(), calls=%async_computation.29 | async-start | bytes 4792320 | tf_op jit(solution)/shard_map/all_gather | solution.py:19
  8.7 300.9 %all-gather.7.cloned.1.call-start = ((), (), s32[]{:S(2)}) async-start(), calls=%async_computation.30 | async-start | bytes 32747520 | tf_op jit(solution)/shard_map/all_gather | solution.py:54
  133.7 17.6 %all-to-all-start = ((bf16[2,128,1152]{2,1,0:T(8,128)(2,1)}), bf16[2,128,1152]{2,1,0:T(8,128)(2,1)}, u32[]{:S(2)}, u32[]{:S(2)}) async-start(bf16[2,128,1152]{2,1,0:T(8,128)(2,1)} %broadcast_in_dim.46), calls=%async_computation | async-start | bytes 1179648 | tf_op jit(solution)/shard_map/all_to_all | solution.py:24
  164.5 19.8 %all-to-all-start.1 = ((f32[2,128,1152]{2,1,0:T(8,128)}), f32[2,128,1152]{2,1,0:T(8,128)S(1)}, u32[]{:S(2)}, u32[]{:S(2)}) async-start(f32[2,128,1152]{2,1,0:T(8,128)} %fusion.33), calls=%async_computation.1 | async-start | bytes 2359296 | tf_op jit(solution)/shard_map/all_to_all | solution.py:45
  168.9 169.3 %copy-start.39 = (f32[1152]{0:T(1024)}, f32[1152]{0:T(1024)S(1)}, u32[]{:S(2)}) copy-start(f32[1152]{0:T(1024)S(1)} %convert_add_fusion.2) | copy-start | bytes 13828
  184.9 209.5 %copy-start.4 = (f32[128,1152]{1,0:T(8,128)}, f32[128,1152]{1,0:T(8,128)S(1)}, u32[]{:S(2)}) copy-start(f32[128,1152]{1,0:T(8,128)S(1)} %get-tuple-element.37) | copy-start | bytes 1769476
  184.9 261.2 %copy-start.56 = (f32[128]{0:T(128)}, f32[128]{0:T(128)S(1)}, u32[]{:S(2)}) copy-start(f32[128]{0:T(128)S(1)} %add_rsqrt_fusion.3) | copy-start | bytes 1540
  456.2 11.6 all-to-all-start.6
  467.9 41.8 %all-to-all-start.27 = ((bf16[64,1,18]{2,1,0:T(2,128)(2,1)}), bf16[64,1,18]{2,1,0:T(2,128)(2,1)}, u32[]{:S(2)}, u32[]{:S(2)}) async-start(bf16[64,1,18]{2,1,0:T(2,128)(2,1)} %convert_element_type.331), calls=%async_computation.27 | async-start | bytes 65536 | tf_op jit(solution)/shard_map/all_to_all | solution.py:361
  509.7 13.1 %all-to-all-start.20 = ((bf16[64,1,18]{2,1,0:T(2,128)(2,1)}), bf16[64,1,18]{2,1,0:T(2,128)(2,1)}, u32[]{:S(2)}, u32[]{:S(2)}) async-start(bf16[64,1,18]{2,1,0:T(2,128)(2,1)} %convert_element_type.329), calls=%async_computation.20 | async-start | bytes 65536 | tf_op jit(solution)/shard_map/all_to_all | solution.py:326
  522.7 13.3 %all-to-all-start.25 = ((bf16[64,1,18]{2,1,0:T(2,128)(2,1)}), bf16[64,1,18]{2,1,0:T(2,128)(2,1)}, u32[]{:S(2)}, u32[]{:S(2)}) async-start(bf16[64,1,18]{2,1,0:T(2,128)(2,1)} %convert_element_type.330), calls=%async_computation.25 | async-start | bytes 65536 | tf_op jit(solution)/shard_map/all_to_all | solution.py:354
  536.0 13.3 %all-to-all-start.7 = ((bf16[2,128,1152]{2,1,0:T(8,128)(2,1)}), bf16[2,128,1152]{2,1,0:T(8,128)(2,1)S(1)}, u32[]{:S(2)}, u32[]{:S(2)}) async-start(bf16[2,128,1152]{2,1,0:T(8,128)(2,1)} %bitcast.119), calls=%async_computation.7 | async-start | bytes 1179648 | tf_op jit(solution)/shard_map/all_to_all | solution.py:63
  549.3 13.2 %all-to-all-start.14 = ((bf16[64,1,4]{2,1,0:T(2,128)(2,1)}), bf16[64,1,4]{2,1,0:T(2,128)(2,1)S(1)}, u32[]{:S(2)}, u32[]{:S(2)}) async-start(bf16[64,1,4]{2,1,0:T(2,128)(2,1)} %convert_element_type.326), calls=%async_computation.14 | async-start | bytes 65536 | tf_op jit(solution)/shard_map/all_to_all | solution.py:305
  562.5 12.6 all-to-all-start.16
  575.1 13.0 %all-to-all-start.18 = ((bf16[64,1,18]{2,1,0:T(2,128)(2,1)}), bf16[64,1,18]{2,1,0:T(2,128)(2,1)S(1)}, u32[]{:S(2)}, u32[]{:S(2)}) async-start(bf16[64,1,18]{2,1,0:T(2,128)(2,1)} %convert_element_type.328), calls=%async_computation.18 | async-start | bytes 65536 | tf_op jit(solution)/shard_map/all_to_all | solution.py:319
  588.7 7.2 all-to-all-start.28
  631.4 26.3 %all-to-all-start.9 = ((bf16[64,18,256]{2,1,0:T(8,128)(2,1)}), bf16[64,18,256]{2,1,0:T(8,128)(2,1)S(1)}, u32[]{:S(2)}, u32[]{:S(2)}) async-start(bf16[64,18,256]{2,1,0:T(8,128)(2,1)} %copy.281), calls=%async_computation.9 | async-start | bytes 1572864 | tf_op jit(solution)/shard_map/all_to_all | solution.py:284
  657.7 19.3 %all-to-all-start.11 = ((bf16[64,18,256]{2,1,0:T(8,128)(2,1)}), bf16[64,18,256]{2,1,0:T(8,128)(2,1)S(1)}, u32[]{:S(2)}, u32[]{:S(2)}) async-start(bf16[64,18,256]{2,1,0:T(8,128)(2,1)} %copy.284), calls=%async_computation.11 | async-start | bytes 1572864 | tf_op jit(solution)/shard_map/all_to_all | solution.py:291
  677.7 7.5 all-to-all-start.10
  685.8 7.5 all-to-all-start.12
  693.9 29.5 %all-to-all-start.8 = ((bf16[64,18,512]{2,1,0:T(8,128)(2,1)}), bf16[64,18,512]{2,1,0:T(8,128)(2,1)S(1)}, u32[]{:S(2)}, u32[]{:S(2)}) async-start(bf16[64,18,512]{2,1,0:T(8,128)(2,1)} %copy.278), calls=%async_computation.8 | async-start | bytes 3145728 | tf_op jit(solution)/shard_map/all_to_all | solution.py:277
  723.4 30.7 %all-to-all-start.13 = ((bf16[64,18,512]{2,1,0:T(8,128)(2,1)}), bf16[64,18,512]{2,1,0:T(8,128)(2,1)}, u32[]{:S(2)}, u32[]{:S(2)}) async-start(bf16[64,18,512]{2,1,0:T(8,128)(2,1)} %copy.289), calls=%async_computation.13 | async-start | bytes 3145728 | tf_op jit(solution)/shard_map/all_to_all | solution.py:298
  754.1 175.6 %all-to-all-start.24 = ((bf16[64,18,3456]{2,1,0:T(8,128)(2,1)}), bf16[64,18,3456]{2,1,0:T(8,128)(2,1)}, u32[]{:S(2)}, u32[]{:S(2)}) async-start(bf16[64,18,3456]{2,1,0:T(8,128)(2,1)} %copy.305), calls=%async_computation.24 | async-start | bytes 21233664 | tf_op jit(solution)/shard_map/all_to_all | solution.py:347
  929.6 175.2 %all-to-all-start.22 = ((bf16[64,18,3456]{2,1,0:T(8,128)(2,1)}), bf16[64,18,3456]{2,1,0:T(8,128)(2,1)}, u32[]{:S(2)}, u32[]{:S(2)}) async-start(bf16[64,18,3456]{2,1,0:T(8,128)(2,1)} %copy.300), calls=%async_computation.22 | async-start | bytes 21233664 | tf_op jit(solution)/shard_map/all_to_all | solution.py:333
  957.5 157.7 %copy-start.65 = (bf16[2,1,18]{2,1,0:T(2,128)(2,1)S(1)}, bf16[2,1,18]{2,1,0:T(2,128)(2,1)}, u32[]{:S(2)}) copy-start(bf16[2,1,18]{2,1,0:T(2,128)(2,1)} %all_to_all.162) | copy-start | bytes 220
  957.5 158.2 %copy-start.66 = (bf16[2,1,4]{2,1,0:T(2,128)(2,1)S(1)}, bf16[2,1,4]{2,1,0:T(2,128)(2,1)}, u32[]{:S(2)}) copy-start(bf16[2,1,4]{2,1,0:T(2,128)(2,1)} %all_to_all.163) | copy-start | bytes 52
  957.5 158.7 %copy-start.67 = (bf16[2,1,4]{2,1,0:T(2,128)(2,1)S(1)}, bf16[2,1,4]{2,1,0:T(2,128)(2,1)}, u32[]{:S(2)}) copy-start(bf16[2,1,4]{2,1,0:T(2,128)(2,1)} %all_to_all.164) | copy-start | bytes 52
  957.5 159.3 %copy-start.68 = (f32[128]{0:T(128)S(1)}, f32[128]{0:T(128)}, u32[]{:S(2)}) copy-start(f32[128]{0:T(128)} %get-tuple-element.26) | copy-start | bytes 1540
  957.5 159.3 %copy-start.11 = (f32[128,1152]{1,0:T(8,128)S(1)}, f32[128,1152]{1,0:T(8,128)}, u32[]{:S(2)}) copy-start(f32[128,1152]{1,0:T(8,128)} %copy-done.10) | copy-start | bytes 1769476
  957.5 160.3 %copy-start.63 = (bf16[2,1,18]{2,1,0:T(2,128)(2,1)S(1)}, bf16[2,1,18]{2,1,0:T(2,128)(2,1)}, u32[]{:S(2)}) copy-start(bf16[2,1,18]{2,1,0:T(2,128)(2,1)} %all_to_all.165) | copy-start | bytes 220
  957.5 161.4 %copy-start.41 = (bf16[2,18,256]{2,1,0:T(8,128)(2,1)S(1)}, bf16[2,18,256]{2,1,0:T(8,128)(2,1)}, u32[]{:S(2)}) copy-start(bf16[2,18,256]{2,1,0:T(8,128)(2,1)} %copy-done.40) | copy-start | bytes 55300
  1104.9 175.3 %all-to-all-start.23 = ((bf16[64,18,3456]{2,1,0:T(8,128)(2,1)}), bf16[64,18,3456]{2,1,0:T(8,128)(2,1)}, u32[]{:S(2)}, u32[]{:S(2)}) async-start(bf16[64,18,3456]{2,1,0:T(8,128)(2,1)} %copy.302), calls=%async_computation.23 | async-start | bytes 21233664 | tf_op jit(solution)/shard_map/all_to_all | solution.py:340
  (65 other events, 1558.9 us)
Sparse Core Ops, SparseCore 0:
  10.3 106.4 all-gather.4
  118.5 190.9 all-gather.6
where the time goes:
time: 1300 us; the launch traced here: 1290 us
  waiting for transfers between devices  641 us (49%)
  blocking collectives  207 us (16%)
  starting transfers between devices  164 us (13%)
  local copies, waits for them, and re-layouts  128 us (10%)
  matrix products  79 us (6%)
  other arithmetic  57.4 us (4%)
  between operations  17.7 us (1%)
    all_to_all x1, waiting for transfers between devices, local(): lax.all_to_all(split_rows(every_term[8], shard_count).astype(jnp.bfloat16...  147 us
    all_to_all x1, waiting for transfers between devices, local(): lax.all_to_all(split_rows(every_term[10], shard_count).astype(jnp.bfloat1...  145 us
    all_to_all x1, waiting for transfers between devices, local(): lax.all_to_all(split_rows(every_term[9], shard_count).astype(jnp.bfloat16...  144 us
    all_gather x1, waiting for transfers between devices, sent_together(): result = lax.all_gather(both, axis, axis=dim, tiled=True)  125 us
    unnamed x1, blocking collectives  112 us
    all_to_all x7, blocking collectives, copy_for_each(): return lax.all_to_all(copies, axis, split_axis=0, concat_axis=0, tiled=True)  60.8 us
    unnamed x161, local copies, waits for them, and re-layouts  51.6 us
    all_to_all x2, blocking collectives, sent_and_summed(): pieces = lax.all_to_all(split_up(value, dim, count), axis, 0, 0, tiled=True)  34 us
  transfers between devices with their start and end apart: 22, of which 18 were waited for; matrix products, arithmetic and copies ran while one was open for 13% of the time, Pallas kernels for 0%

commit v1 on v0

v1 whole, which is shorter than its diff:
```python
import functools
import math

import jax
import jax.numpy as jnp
from jax import lax
from jax.experimental import pallas as pl
from jax.experimental.pallas import tpu as pltpu
from jax.sharding import PartitionSpec as P

eps = 1e-06
gelu_scale = 0.7978845608028654
gelu_cube = 0.044715


def rms_apply(values, gain_vec):
    inverse = lax.rsqrt(jnp.mean(values * values, axis=-1, keepdims=True) + eps)
    return (values * inverse * (1.0 + gain_vec), inverse)


def rms_back(values, inverse, gain_vec, grad_out):
    scaled = grad_out * (1.0 + gain_vec)
    grad_value = inverse * scaled - values * inverse * inverse * inverse * jnp.mean(
        scaled * values, axis=-1, keepdims=True
    )
    grad_gain = jnp.sum(grad_out * values * inverse, axis=tuple(range(values.ndim - 1)))
    return (grad_value, grad_gain)


def positions_of(segment_row):
    token_index = jnp.arange(segment_row.shape[0], dtype=jnp.int32)
    earlier = jnp.concatenate([segment_row[:1] - 1, segment_row[:-1]])
    starts = lax.cummax(jnp.where(segment_row != earlier, token_index, 0), axis=0)
    return token_index - starts


def build_allowed(segment_row):
    token_index = jnp.arange(segment_row.shape[0], dtype=jnp.int32)
    same_seq = segment_row[:, None] == segment_row[None, :]
    causal = token_index[None, :] <= token_index[:, None]
    return same_seq & causal


def rope_tables(position, width):
    half_width = width // 2
    frequency = jnp.exp(
        jnp.arange(half_width, dtype=jnp.float32) * (-2.0 * math.log(10000.0) / width)
    )
    angles = position.astype(jnp.float32)[:, None] * frequency[None, :]
    cosine_table = jnp.concatenate([jnp.cos(angles), jnp.cos(angles)], axis=1)
    sine_table = jnp.concatenate([jnp.sin(angles), jnp.sin(angles)], axis=1)
    return (cosine_table, sine_table)


def rotate_half(values):
    half_width = values.shape[-1] // 2
    return jnp.concatenate([-values[..., half_width:], values[..., :half_width]], axis=-1)


f32 = jnp.float32
bf16 = jnp.bfloat16
MESH = pl.DeviceIdType.MESH
ROWS = 144
SHARD = 18
VMEM_SPEC = pl.BlockSpec(memory_space=pltpu.VMEM)
ANY_SPEC = pl.BlockSpec(memory_space=pl.ANY)
VMEM_MOST = 66_000_000

CLASSES = (
    (0, 2, "zxy"),
    (2, 4, "zyx"),
    (4, 6, "xyz"),
    (6, 8, "yxz"),
    (8, 10, "zxy"),
    (10, 12, "zyx"),
)


def coords():
    dp, t = lax.axis_index("dp"), lax.axis_index("tensor")
    return {"c": lax.rem(dp, 2), "y": lax.rem(dp // 2, 4), "x": lax.rem(dp // 8, 4), "z": dp // 32, "t": t}


def device(at, **change):
    p = {**at, **change}
    return (((p["z"] * 4 + p["x"]) * 4 + p["y"]) * 2 + p["c"], p["t"])


def ahead(at, dim, by):
    size = 2 if dim == "z" else 4
    return lax.rem(at[dim] + by + size, size)


def block_sources():
    attn = [("q", j) for j in range(4)] + [("k", j) for j in range(2)]
    attn_two = [("v", j) for j in range(2)] + [("o", j) for j in range(4)]
    ffn = [[(n, j) for n in "gud" for j in range(14)], [(n, j + 14) if j < 13 else None for n in "gud" for j in range(14)]]
    return [attn + ffn[0], attn_two + ffn[1]]


def enter(peers):
    barrier = pltpu.get_barrier_semaphore()
    for peer in peers:
        pl.semaphore_signal(barrier, inc=1, device_id=peer, device_id_type=MESH)
    pl.semaphore_wait(barrier, len(peers))


def remote(src, dst, send, recv, to):
    return pltpu.make_async_remote_copy(
        src_ref=src, dst_ref=dst, send_sem=send, recv_sem=recv, device_id=to, device_id_type=MESH
    )


def group_peers(at):
    peers = []
    for dy in range(4):
        for dc in range(2):
            if dy or dc:
                peers.append({**at, "y": ahead(at, "y", dy), "c": lax.rem(at["c"] + dc, 2)})
    return peers


def slot_of(p):
    return p["c"] * 4 + p["y"]


def part_of(buf, at, done, dim, index, i0, i1):
    pick = {d: (slice(None) if d in done else at[d]) for d in "zxy"}
    if dim is not None:
        pick[dim] = index
    return buf.at[pick["y"], i0:i1, pick["z"], pick["x"]]


def size_of(done, n):
    size = n * ROWS * 128 * 2
    for d in done:
        size *= 2 if d == "z" else 4
    return size


def order_gather(classes, rate=46e3, hop=1.6):
    free, events, queue = {}, [], []
    for k, (i0, i1, order) in enumerate(classes):
        queue.append((0.0, k, 0, 0))
    while queue:
        queue.sort()
        ready, k, ph, st = queue.pop(0)
        i0, i1, order = classes[k]
        events.append((k, ph, st))
        if ph == len(order):
            continue
        dim, done = order[ph], order[:ph]
        size = size_of(done, i1 - i0)
        if dim == "z":
            ways, moved, follow = ("z+",), size, (k, ph + 1, 0)
        elif st == 0:
            ways, moved, follow = (dim + "+", dim + "-"), size, (k, ph, 1)
        else:
            ways, moved, follow = (dim + "+", dim + "-"), size / 2, (k, ph + 1, 0)
        end = 0.0
        for way in ways:
            free[way] = max(ready, free.get(way, 0.0)) + moved / rate
            end = max(end, free[way])
        queue.append((end + hop, *follow))
    return events


def gather_kernel(
    q_ref, k_ref, v_ref, o_ref, g_ref, u_ref, d_ref, gains_ref, tok_ref,
    buf, other, gbuf, tok_out,
    send, got, own32, own, ggot, gmine,
    a_send, a_recv, g_send, g_recv, s_sem, r_sem, e_sem, l_sem,
):
    at = coords()
    refs = {"q": q_ref, "k": k_ref, "v": v_ref, "o": o_ref, "g": g_ref, "u": u_ref, "d": d_ref}
    group = group_peers(at)
    partner = device(at, c=1 - at["c"])
    mirror = device(at, t=1 - at["t"])
    ring = [device(at, x=ahead(at, "x", 1)), device(at, x=ahead(at, "x", -1)), device(at, z=1 - at["z"])]
    for k, blocks in enumerate(block_sources()):
        for pos, source in enumerate(blocks):
            y, i = divmod(pos, 12)
            if source is None:
                send[k * 4 + y, i] = jnp.zeros((SHARD, 128), bf16)
            else:
                name, j = source
                send[k * 4 + y, i] = refs[name][:, j * 128 : (j + 1) * 128]
    row = lax.broadcasted_iota(jnp.int32, (8, 128), 0)
    gmine[...] = jnp.where(row == at["y"] * 2 + at["c"], gains_ref[...], 0.0)
    me = slot_of(at)
    mine = at["y"] * 2 + at["c"]
    enter([device(p) for p in group] + ring + [mirror])
    tok = remote(tok_ref, tok_out.at[at["t"]], e_sem.at[2], e_sem.at[3], mirror)
    tok.start()
    tok_local = pltpu.make_async_copy(tok_ref, tok_out.at[at["t"]], l_sem.at[1])
    tok_local.start()
    first = []
    for n, p in enumerate(group):
        copy = remote(send.at[slot_of(p)], got.at[mine], a_send.at[n], a_recv.at[mine], device(p))
        small = remote(gmine, ggot.at[mine], g_send.at[n], g_recv.at[mine], device(p))
        copy.start()
        small.start()
        first += [copy, small]
    here = pltpu.make_async_copy(send.at[me], got.at[mine], l_sem.at[0])
    here.start()
    here.wait()
    for p in group:
        s = p["y"] * 2 + p["c"]
        remote(send.at[0], got.at[s], a_send.at[0], a_recv.at[s], device(p)).wait_recv()
        remote(gmine, ggot.at[s], g_send.at[0], g_recv.at[s], device(p)).wait_recv()
    ggot[mine] = gmine[...]
    gmine_sum = ggot[0]
    for s in range(1, 8):
        gmine_sum = gmine_sum + ggot[s]

    @pl.loop(0, 12)
    def _(i):
        for s in range(8):
            own32[SHARD * s : SHARD * (s + 1), :] = got[s, i].astype(f32)
        own[i] = own32[...].astype(bf16)

    for copy in first:
        copy.wait_send()
    gmine[...] = gmine_sum
    local = pltpu.make_async_copy(own, part_of(buf, at, "", None, None, 0, 12), l_sem.at[0])
    local.start()
    glocal = pltpu.make_async_copy(gmine, gbuf.at[at["z"], at["x"]], l_sem.at[2])
    glocal.start()
    pending = []

    def incoming(k, ph, st):
        i0, i1, order = CLASSES[k]
        dim, done = order[ph], order[:ph]
        half = (i1 - i0) // 2
        if dim == "z":
            return [(part_of(buf, at, done, "z", 1 - at["z"], i0, i1), r_sem.at[k, ph, 0])]
        left, right = ahead(at, dim, -1), ahead(at, dim, 1)
        if st == 0:
            return [
                (part_of(buf, at, done, dim, left, i0, i1), r_sem.at[k, ph, 0]),
                (part_of(buf, at, done, dim, right, i0, i1), r_sem.at[k, ph, 1]),
            ]
        across = ahead(at, dim, 2)
        return [
            (part_of(buf, at, done, dim, across, i0, i0 + half), r_sem.at[k, ph, 2]),
            (part_of(buf, at, done, dim, across, i0 + half, i1), r_sem.at[k, ph, 3]),
        ]

    def await_step(k, ph, st):
        for ref, sem in incoming(k, ph, st):
            remote(ref, ref, s_sem.at[k, ph, 0], sem, partner).wait_recv()

    local_waited = []

    def push(ref_from, ref_to, k, ph, n, to):
        copy = remote(ref_from, ref_to, s_sem.at[k, ph, n], r_sem.at[k, ph, n], to)
        copy.start()
        pending.append(copy)

    def gpush(src, dst, n, to):
        copy = remote(src, dst, g_send.at[8 + n], g_recv.at[8 + n], to)
        copy.start()
        pending.append(copy)

    xr, xl = device(at, x=ahead(at, "x", 1)), device(at, x=ahead(at, "x", -1))
    zo = device(at, z=1 - at["z"])
    gpush(gmine, gbuf.at[at["z"], at["x"]], 0, xr)
    gpush(gmine, gbuf.at[at["z"], at["x"]], 1, xl)

    def gwait(x, z, n):
        ref = gbuf.at[z, x]
        remote(ref, ref, g_send.at[0], g_recv.at[8 + n], partner).wait_recv()

    for k, ph, st in order_gather(CLASSES):
        i0, i1, order = CLASSES[k]
        if st == 1:
            await_step(k, ph, 0)
        elif ph > 0:
            await_step(k, ph - 1, 0 if order[ph - 1] == "z" else 1)
        if ph == 3:
            continue
        dim, done = order[ph], order[:ph]
        half = (i1 - i0) // 2
        if ph > 0 and not local_waited:
            local.wait()
            local_waited.append(1)

        def mine_part(lo, hi):
            if ph == 0:
                return own.at[lo:hi]
            return part_of(buf, at, done, dim, at[dim], lo, hi)

        target = part_of(buf, at, done, dim, at[dim], i0, i1)
        if dim == "z":
            push(mine_part(i0, i1), target, k, ph, 0, zo)
            continue
        right, left = device(at, **{dim: ahead(at, dim, 1)}), device(at, **{dim: ahead(at, dim, -1)})
        if st == 0:
            push(mine_part(i0, i1), target, k, ph, 0, right)
            push(mine_part(i0, i1), target, k, ph, 1, left)
        else:
            a = part_of(buf, at, done, dim, ahead(at, dim, -1), i0, i0 + half)
            b = part_of(buf, at, done, dim, ahead(at, dim, 1), i0 + half, i1)
            push(a, a, k, ph, 2, right)
            push(b, b, k, ph, 3, left)
    swap = remote(buf.at[0, 0:6], other, e_sem.at[0], e_sem.at[1], partner)
    swap.start()
    glocal.wait()
    gwait(ahead(at, "x", -1), at["z"], 0)
    gwait(ahead(at, "x", 1), at["z"], 1)
    fwd = gbuf.at[at["z"], ahead(at, "x", -1)]
    gpush(fwd, fwd, 2, xr)
    gwait(ahead(at, "x", 2), at["z"], 2)
    gpush(gbuf.at[at["z"]], gbuf.at[at["z"]], 3, zo)
    ref = gbuf.at[1 - at["z"]]
    remote(ref, ref, g_send.at[0], g_recv.at[11], partner).wait_recv()
    for copy in pending:
        copy.wait_send()
    tok_local.wait()
    tok.wait_send()
    ref = tok_out.at[1 - at["t"]]
    remote(ref, ref, e_sem.at[2], e_sem.at[3], partner).wait_recv()
    swap.wait()


def gather_all(w, gains, tokens):
    n = len(CLASSES)
    dma = pltpu.SemaphoreType.DMA
    return pl.pallas_call(
        gather_kernel,
        name="gather_weights",
        out_shape=(
            jax.ShapeDtypeStruct((4, 12, 2, 4, ROWS, 128), bf16),
            jax.ShapeDtypeStruct((6, 2, 4, ROWS, 128), bf16),
            jax.ShapeDtypeStruct((2, 4, 8, 128), f32),
            jax.ShapeDtypeStruct((2, *tokens.shape), bf16),
        ),
        in_specs=[VMEM_SPEC] * 9,
        out_specs=[ANY_SPEC] * 4,
        scratch_shapes=[
            pltpu.VMEM((8, 12, SHARD, 128), bf16),
            pltpu.VMEM((8, 12, SHARD, 128), bf16),
            pltpu.VMEM((ROWS, 128), f32),
            pltpu.VMEM((12, ROWS, 128), bf16),
            pltpu.VMEM((8, 8, 128), f32),
            pltpu.VMEM((8, 128), f32),
            dma((8,)),
            dma((8,)),
            dma((12,)),
            dma((12,)),
            dma((n, 3, 4)),
            dma((n, 3, 4)),
            dma((4,)),
            dma((3,)),
        ],
        compiler_params=pltpu.CompilerParams(collective_id=1, has_side_effects=True, vmem_limit_bytes=VMEM_MOST),
    )(*w, gains, tokens)


def order_scatter(classes, rate=46e3, hop=2.5):
    free, events, queue = {}, [], []
    for k in range(len(classes)):
        queue.append((0.0, k, 0, 0))
    while queue:
        queue.sort()
        ready, k, ph, st = queue.pop(0)
        i0, i1, order = classes[k]
        events.append((k, ph, st))
        if ph == len(order):
            continue
        dim, done = order[2 - ph], order[: 2 - ph]
        size = size_of(done, i1 - i0)
        if dim == "z":
            ways, moved, follow = ("z+",), size, (k, ph + 1, 0)
        elif st == 0:
            ways, moved, follow = (dim + "+", dim + "-"), size / 2, (k, ph, 1)
        else:
            ways, moved, follow = (dim + "+", dim + "-"), size, (k, ph + 1, 0)
        end = 0.0
        for way in ways:
            begin = max(ready, free.get(way, 0.0))
            free[way] = begin + (size if dim != "z" and st == 0 else moved if dim == "z" else size / 2) / rate
            end = max(end, begin + (moved if st == 0 else size / 2) / rate)
        queue.append((end + hop, *follow))
    return events


def recv_shape(done, n):
    return (*((4,) if "y" in done else ()), n, *((2,) if "z" in done else ()), *((4,) if "x" in done else ()), ROWS, 128)


def scatter_shapes():
    shapes = []
    for i0, i1, order in CLASSES:
        n = i1 - i0
        for ph in range(3):
            dim, done = order[2 - ph], order[: 2 - ph]
            if dim == "z":
                shapes.append(recv_shape(done, n))
            else:
                shapes.append((4, *recv_shape(done, n // 2)))
                shapes.append((2, *recv_shape(done, n // 2)))
    return shapes


def add_into(acc_part, refs):
    shape = acc_part.shape[:-2]
    total = math.prod(shape)

    @pl.loop(0, total)
    def _(at):
        index, rest = [], at
        for size in reversed(shape):
            index.insert(0, lax.rem(rest, size))
            rest = rest // size
        value = acc_part[tuple(index)].astype(f32)
        for ref in refs:
            value = value + ref[tuple(index)].astype(f32)
        acc_part[tuple(index)] = value.astype(bf16)


def scatter_kernel(
    attn_own, attn_other, ffn, gains,
    q_out, k_out, v_out, o_out, g_out, u_out, d_out, gains_out,
    acc, pair, own32, send, got, gacc, grecv, ggot, kv, kvr, gfin, gfinal, gother, *rest,
):
    lands, (s_sem, r_sem, a_send, a_recv, g_send, g_recv, e_sem, l_sem) = rest[:-8], rest[-8:]
    at = coords()
    group = group_peers(at)
    partner = device(at, c=1 - at["c"])
    mirror = device(at, t=1 - at["t"])
    ring = [device(at, x=ahead(at, "x", 1)), device(at, x=ahead(at, "x", -1)), device(at, z=1 - at["z"])]
    ring.append(device(at, x=ahead(at, "x", 2)))
    loads = []
    for y in range(4):
        if y == 0:
            loads.append(pltpu.make_async_copy(attn_own, acc.at[0, 0:6], l_sem.at[0]))
            loads.append(pltpu.make_async_copy(ffn.at[0:6], acc.at[0, 6:12], l_sem.at[1]))
        else:
            loads.append(pltpu.make_async_copy(ffn.at[12 * y - 6 : 12 * y + 6], acc.at[y], l_sem.at[y + 1]))
    loads.append(pltpu.make_async_copy(gains, gacc, l_sem.at[5]))
    for copy in loads:
        copy.start()
    enter([device(p) for p in group] + ring + [mirror])
    swap = remote(attn_other, pair, e_sem.at[0], e_sem.at[1], partner)
    swap.start()
    pending = []

    def push(src, dst, send_sem, recv_sem, to):
        copy = remote(src, dst, send_sem, recv_sem, to)
        copy.start()
        pending.append(copy)

    for copy in loads:
        copy.wait()
    swap.wait()
    add_into(acc.at[0, 0:6], [pair])

    zo = device(at, z=1 - at["z"])
    push(gacc.at[1 - at["z"]], grecv.at[0:4], g_send.at[8], g_recv.at[8], zo)

    slots, position = {}, 0
    for k, (i0, i1, order) in enumerate(CLASSES):
        for ph in range(3):
            if order[2 - ph] == "z":
                slots[k, ph] = (lands[position],)
                position += 1
            else:
                slots[k, ph] = (lands[position], lands[position + 1])
                position += 2

    def await_ref(ref, sem):
        remote(ref, ref, s_sem.at[0, 0, 0], sem, partner).wait_recv()

    for k, ph, st in order_scatter(CLASSES):
        i0, i1, order = CLASSES[k]
        half = (i1 - i0) // 2
        if st == 0 and ph > 0:
            dim, done = order[3 - ph], order[: 3 - ph]
            if dim == "z":
                (land,) = slots[k, ph - 1]
                await_ref(land, r_sem.at[k, ph - 1, 0])
                add_into(part_of(acc, at, done, "z", at["z"], i0, i1), [land])
            else:
                wide, _ = slots[k, ph - 1]
                for n in range(4):
                    await_ref(wide.at[n], r_sem.at[k, ph - 1, 2 + n])
                add_into(part_of(acc, at, done, dim, at[dim], i0, i0 + half), [wide.at[0], wide.at[2]])
                add_into(part_of(acc, at, done, dim, at[dim], i0 + half, i1), [wide.at[1], wide.at[3]])
        if ph == 3:
            continue
        dim, done = order[2 - ph], order[: 2 - ph]
        if dim == "z":
            (land,) = slots[k, ph]
            push(part_of(acc, at, done, "z", 1 - at["z"], i0, i1), land, s_sem.at[k, ph, 0], r_sem.at[k, ph, 0], zo)
            continue
        right, left = device(at, **{dim: ahead(at, dim, 1)}), device(at, **{dim: ahead(at, dim, -1)})
        wide, narrow = slots[k, ph]
        p1, m1, p2 = ahead(at, dim, 1), ahead(at, dim, -1), ahead(at, dim, 2)
        lo, hi = (i0, i0 + half), (i0 + half, i1)

        def sem(n):
            return s_sem.at[k, ph, n], r_sem.at[k, ph, n]

        if st == 0:
            push(part_of(acc, at, done, dim, p2, *lo), narrow.at[0], *sem(0), right)
            push(part_of(acc, at, done, dim, p2, *hi), narrow.at[1], *sem(1), left)
            push(part_of(acc, at, done, dim, p1, *hi), wide.at[1], *sem(3), right)
            push(part_of(acc, at, done, dim, m1, *lo), wide.at[2], *sem(4), left)
        else:
            await_ref(narrow.at[0], r_sem.at[k, ph, 0])
            add_into(part_of(acc, at, done, dim, p1, *lo), [narrow.at[0]])
            push(part_of(acc, at, done, dim, p1, *lo), wide.at[0], *sem(2), right)
            await_ref(narrow.at[1], r_sem.at[k, ph, 1])
            add_into(part_of(acc, at, done, dim, m1, *hi), [narrow.at[1]])
            push(part_of(acc, at, done, dim, m1, *hi), wide.at[3], *sem(5), left)

    await_ref(grecv.at[0:4], g_recv.at[8])
    gacc[at["z"]] = gacc[at["z"]] + grecv[0:4]
    for n in range(1, 4):
        xx = ahead(at, "x", n)
        push(gacc.at[at["z"], xx], grecv.at[4 + n], g_send.at[8 + n], g_recv.at[8 + n], device(at, x=xx))

    mine = at["y"] * 2 + at["c"]
    me = slot_of(at)

    @pl.loop(0, 12)
    def _(i):
        own32[...] = acc[at["y"], i, at["z"], at["x"]].astype(f32)
        for s in range(8):
            send[s, i] = own32[SHARD * s : SHARD * (s + 1), :].astype(bf16)

    for n, p in enumerate(group):
        s = p["y"] * 2 + p["c"]
        push(send.at[s], got.at[me], a_send.at[n], a_recv.at[me], device(p))
    here = pltpu.make_async_copy(send.at[mine], got.at[me], l_sem.at[0])
    here.start()
    gsum = gacc[at["z"], at["x"]]
    for n in range(1, 4):
        await_ref(grecv.at[4 + n], g_recv.at[8 + n])
        gsum = gsum + grecv[4 + n]
    gfin[...] = gsum
    for n, p in enumerate(group):
        push(gfin, ggot.at[mine], g_send.at[n], g_recv.at[mine], device(p))
    here.wait()
    for p in group:
        ref = got.at[slot_of(p)]
        await_ref(ref, a_recv.at[slot_of(p)])
    ggot[mine] = gsum
    for p in group:
        s = p["y"] * 2 + p["c"]
        await_ref(ggot.at[s], g_recv.at[s])
    total = ggot[0]
    for s in range(1, 8):
        total = total + ggot[s]
    gfinal[...] = total
    outs = {"q": q_out, "o": o_out, "g": g_out, "u": u_out, "d": d_out}
    later = []
    for k, blocks in enumerate(block_sources()):
        for pos, source in enumerate(blocks):
            if source is None:
                continue
            y, i = divmod(pos, 12)
            name, j = source
            if name in "kv":
                j += 2 if name == "v" else 0
                kv[:, j * 128 : (j + 1) * 128] = got[k * 4 + y, i].astype(f32)
            else:
                later.append((name, j, k * 4 + y, i))
    push(kv, kvr, e_sem.at[2], e_sem.at[3], mirror)
    push(gfinal, gother, e_sem.at[4], e_sem.at[5], mirror)
    for name, j, s, i in later:
        outs[name][:, j * 128 : (j + 1) * 128] = got[s, i].astype(f32)
    await_ref(kvr, e_sem.at[3])
    await_ref(gother, e_sem.at[5])
    k_out[...] = kv[:, 0:256] + kvr[:, 0:256]
    v_out[...] = kv[:, 256:512] + kvr[:, 256:512]
    gains_out[...] = gfinal[...] + gother[...]
    for copy in pending:
        copy.wait_send()


def scatter_all(attn_own, attn_other, ffn, gains):
    n = len(CLASSES)
    dma = pltpu.SemaphoreType.DMA
    widths = (512, 256, 256, 512, 3456, 3456, 3456)
    return pl.pallas_call(
        scatter_kernel,
        name="scatter_grads",
        out_shape=tuple(jax.ShapeDtypeStruct((SHARD, w), f32) for w in widths) + (jax.ShapeDtypeStruct((8, 128), f32),),
        in_specs=[ANY_SPEC] * 4,
        out_specs=[VMEM_SPEC] * 8,
        scratch_shapes=[
            pltpu.VMEM((4, 12, 2, 4, ROWS, 128), bf16),
            pltpu.VMEM((6, 2, 4, ROWS, 128), bf16),
            pltpu.VMEM((ROWS, 128), f32),
            pltpu.VMEM((8, 12, SHARD, 128), bf16),
            pltpu.VMEM((8, 12, SHARD, 128), bf16),
            pltpu.VMEM((2, 4, 8, 128), f32),
            pltpu.VMEM((8, 8, 128), f32),
            pltpu.VMEM((8, 8, 128), f32),
            pltpu.VMEM((SHARD, 512), f32),
            pltpu.VMEM((SHARD, 512), f32),
            pltpu.VMEM((8, 128), f32),
            pltpu.VMEM((8, 128), f32),
            pltpu.VMEM((8, 128), f32),
            *[pltpu.VMEM(s, bf16) for s in scatter_shapes()],
            dma((n, 3, 6)),
            dma((n, 3, 6)),
            dma((8,)),
            dma((8,)),
            dma((12,)),
            dma((12,)),
            dma((6,)),
            dma((6,)),
        ],
        compiler_params=pltpu.CompilerParams(collective_id=2, has_side_effects=True, vmem_limit_bytes=VMEM_MOST),
    )(attn_own, attn_other, ffn, gains)


def pair_kernel(reduce, src, out, stage, land, send_sem, recv_sem, local_sem):
    at = coords()
    mirror = device(at, t=1 - at["t"])
    mine = pl.ds(pl.multiple_of(at["t"] * 128, 128), 128)
    theirs = pl.ds(pl.multiple_of((1 - at["t"]) * 128, 128), 128)
    if reduce:
        stage[...] = src[theirs, :].astype(bf16)
        enter([mirror])
        copy = remote(stage, land, send_sem, recv_sem, mirror)
        copy.start()
        copy.wait()
        out[...] = src[mine, :] + land[...].astype(f32)
    else:
        enter([mirror])
        copy = remote(src, land, send_sem, recv_sem, mirror)
        copy.start()
        out[mine, :] = src[...]
        copy.wait()
        out[theirs, :] = land[...]


def pair_call(value, reduce, number):
    rows, width = value.shape
    dma = pltpu.SemaphoreType.DMA
    out = (rows // 2, width) if reduce else (rows * 2, width)
    return pl.pallas_call(
        functools.partial(pair_kernel, reduce),
        name="pair_sum" if reduce else "pair_gather",
        out_shape=jax.ShapeDtypeStruct(out, f32 if reduce else bf16),
        in_specs=[VMEM_SPEC],
        out_specs=VMEM_SPEC,
        scratch_shapes=[pltpu.VMEM((128, width), bf16), pltpu.VMEM((128, width), bf16), dma, dma, dma],
        compiler_params=pltpu.CompilerParams(collective_id=number, has_side_effects=True),
    )(value)


def ffn_kernel(
    x_in, res, cot, gain, buf,
    out, d_in, gpp, grads,
    w, dw, xs, ds, xt, dt, gates, ups, part, land_a, land_b, zstage, zland_a, zland_b,
    w_sem, dw_sem, s_sem, r_sem,
):
    at = coords()
    mirror = device(at, t=1 - at["t"])
    partner = device(at, c=1 - at["c"])
    pairs = 7
    loads = []
    for j in range(pairs):
        for n in range(3):
            lo = n * 14 + 2 * j
            copy = pltpu.make_async_copy(buf.at[6 + lo : 8 + lo], w.at[lo : lo + 2], w_sem.at[j, n])
            copy.start()

    def rows(c, t, n=1):
        return pl.ds(pl.multiple_of((c * 2 + t) * 128, 128), 128 * n)

    enter([mirror, partner])
    c, t = at["c"], at["t"]

    def gather(e, full):
        view = lambda cc, tt: full.at[rows(cc, tt), :]
        a = remote(view(c, t), view(c, t), s_sem.at[e, 0], r_sem.at[e, 0], mirror)
        b = remote(view(c, t), view(c, t), s_sem.at[e, 1], r_sem.at[e, 1], partner)
        a.start()
        b.start()
        ref = view(c, 1 - t)
        remote(ref, ref, s_sem.at[e, 0], r_sem.at[e, 0], mirror).wait_recv()
        f = remote(ref, ref, s_sem.at[e, 2], r_sem.at[e, 2], partner)
        f.start()
        one, two = view(1 - c, t), view(1 - c, 1 - t)
        remote(one, one, s_sem.at[e, 0], r_sem.at[e, 1], mirror).wait_recv()
        remote(two, two, s_sem.at[e, 0], r_sem.at[e, 2], mirror).wait_recv()
        for copy in (a, b, f):
            copy.wait_send()

    def reduce(e, land, zland):
        a = remote(part.at[rows(1 - c, 0, 2), :], land, s_sem.at[e, 0], r_sem.at[e, 0], partner)
        a.start()
        a.wait()
        far = pl.ds(pl.multiple_of((1 - t) * 128, 128), 128)
        near = pl.ds(pl.multiple_of(t * 128, 128), 128)
        zstage[...] = (part[rows(c, 1 - t), :] + land[far, :]).astype(bf16)
        b = remote(zstage, zland, s_sem.at[e, 1], r_sem.at[e, 1], mirror)
        b.start()
        kept = part[rows(c, t), :] + land[near, :]
        b.wait()
        return kept + zland[...].astype(f32)

    xs[rows(c, t), :] = x_in[...]
    gather(0, xs)
    part[...] = jnp.zeros_like(part)

    def weights(j, n):
        return jnp.concatenate([w[n * 14 + 2 * j], w[n * 14 + 2 * j + 1]], axis=1)

    def rows_dot(a, b):
        return lax.dot_general(a, b, (((1,), (1,)), ((), ())), preferred_element_type=f32)

    @pl.loop(0, pairs)
    def _(j):
        lanes = pl.ds(pl.multiple_of(j * 256, 256), 256)
        for n in range(3):
            pltpu.make_async_copy(buf.at[0:2], w.at[0:2], w_sem.at[j, n]).wait()
        gate = jnp.dot(xs[...], weights(j, 0), preferred_element_type=f32)
        up = jnp.dot(xs[...], weights(j, 1), preferred_element_type=f32)
        gates[:, lanes] = gate
        ups[:, lanes] = up
        act = 0.5 * gate * (1.0 + jnp.tanh(gelu_scale * (gate + gelu_cube * gate * gate * gate)))
        hidden = (act * up).astype(bf16)
        part[...] += rows_dot(hidden, weights(j, 2))

    raw = reduce(1, land_a, zland_a)
    width = raw.shape[1]
    inverse = lax.rsqrt(jnp.sum(raw * raw, axis=-1, keepdims=True) * (1.0 / width) + eps)
    gained = 1.0 + gain[...]
    out[...] = (res[...] + raw * inverse * gained).astype(bf16)
    g = cot[...].astype(f32)
    scaled = g * gained
    mean = jnp.sum(scaled * raw, axis=-1, keepdims=True) * (1.0 / width)
    ds[rows(c, t), :] = (inverse * scaled - raw * inverse * inverse * inverse * mean).astype(bf16)
    gpp[...] = jnp.sum(g * raw * inverse, axis=0, keepdims=True)
    gather(2, ds)
    xt[...] = xs[...].T
    dt[...] = ds[...].T
    part[...] = jnp.zeros_like(part)

    @pl.loop(0, pairs)
    def _(j):
        lanes = pl.ds(pl.multiple_of(j * 256, 256), 256)
        gate, up = gates[:, lanes], ups[:, lanes]
        d_hidden = jnp.dot(ds[...], weights(j, 2), preferred_element_type=f32)
        tanh = jnp.tanh(gelu_scale * (gate + gelu_cube * gate * gate * gate))
        act = 0.5 * gate * (1.0 + tanh)
        slope = 0.5 * (1.0 + tanh) + 0.5 * gate * (1.0 - tanh * tanh) * gelu_scale * (
            1.0 + 3.0 * gelu_cube * gate * gate
        )
        hidden = (act * up).astype(bf16)
        d_gate = (d_hidden * up * slope).astype(bf16)
        d_up = (d_hidden * act).astype(bf16)
        part[...] += rows_dot(d_gate, weights(j, 0)) + rows_dot(d_up, weights(j, 1))
        for n, (left, right) in enumerate(((xt, d_gate), (xt, d_up), (dt, hidden))):
            grad = jnp.dot(left[...], right, preferred_element_type=f32).astype(bf16)
            lo = n * 14 + 2 * j
            dw[lo] = grad[:, :128]
            dw[lo + 1] = grad[:, 128:]
            pltpu.make_async_copy(dw.at[pl.ds(lo, 2)], grads.at[pl.ds(lo, 2)], dw_sem.at[j, n]).start()

    d_in[...] = reduce(3, land_b, zland_b)
    for j in range(pairs):
        for n in range(3):
            lo = n * 14 + 2 * j
            pltpu.make_async_copy(dw.at[lo : lo + 2], grads.at[lo : lo + 2], dw_sem.at[j, n]).wait()


def ffn_all(x_in, res, cot, gain, buf):
    dma = pltpu.SemaphoreType.DMA
    tokens, width = x_in.shape
    return pl.pallas_call(
        ffn_kernel,
        name="ffn_layer",
        out_shape=(
            jax.ShapeDtypeStruct((tokens, width), bf16),
            jax.ShapeDtypeStruct((tokens, width), f32),
            jax.ShapeDtypeStruct((1, width), f32),
            jax.ShapeDtypeStruct((42, width, 128), bf16),
        ),
        in_specs=[VMEM_SPEC] * 4 + [ANY_SPEC],
        out_specs=[VMEM_SPEC] * 3 + [ANY_SPEC],
        scratch_shapes=[
            pltpu.VMEM((42, width, 128), bf16),
            pltpu.VMEM((42, width, 128), bf16),
            pltpu.VMEM((512, width), bf16),
            pltpu.VMEM((512, width), bf16),
            pltpu.VMEM((width, 512), bf16),
            pltpu.VMEM((width, 512), bf16),
            pltpu.VMEM((512, 1792), f32),
            pltpu.VMEM((512, 1792), f32),
            pltpu.VMEM((512, width), f32),
            pltpu.VMEM((256, width), f32),
            pltpu.VMEM((256, width), f32),
            pltpu.VMEM((128, width), bf16),
            pltpu.VMEM((128, width), bf16),
            pltpu.VMEM((128, width), bf16),
            dma((7, 3)),
            dma((7, 3)),
            dma((4, 3)),
            dma((4, 3)),
        ],
        compiler_params=pltpu.CompilerParams(collective_id=3, has_side_effects=True, vmem_limit_bytes=VMEM_MOST),
    )(x_in, res, cot, gain, buf)


def local(
    tokens,
    segment_ids,
    w_query,
    w_key,
    w_value,
    w_out,
    gain_query,
    gain_key,
    gain_pre_attn,
    gain_post_attn,
    w_gate,
    w_up,
    w_down,
    gain_pre_ffn,
    gain_post_ffn,
    cotangent,
):
    my_dp, my_t = lax.axis_index("dp"), lax.axis_index("tensor")
    core = lax.rem(my_dp, 2)
    packed = jnp.concatenate(
        [gain_pre_attn, gain_post_attn, gain_pre_ffn, gain_post_ffn, gain_query, gain_key]
    ).astype(f32)
    packed = jnp.broadcast_to(jnp.pad(packed, (0, 48))[None], (8, 128))
    buf, other, all_gains, both_tokens = gather_all(
        (w_query, w_key, w_value, w_out, w_gate, w_up, w_down), packed, tokens
    )
    width = tokens.shape[1]
    buf = buf.reshape(48, width, 128)
    mine, other = buf[:6], other.reshape(6, width, 128)

    def matrix(blocks):
        return jnp.moveaxis(blocks, 0, 1).reshape(width, -1)

    first = jnp.where(core == 0, mine, other)
    second = jnp.where(core == 0, other, mine)
    query_mat, key_mat = matrix(first[:4]), matrix(first[4:])
    value_mat, out_mat = matrix(second[:2]), matrix(second[2:])
    all_gains = all_gains.reshape(64, 128)
    gain_pa, gain_po, gain_pf, gain_pp = [all_gains[:, 18 * n : 18 * n + 18].reshape(width) for n in range(4)]
    gain_q, gain_k = [all_gains[:, 72 + 4 * n : 76 + 4 * n].reshape(256) for n in range(2)]
    head_size = key_mat.shape[1]
    heads_local = query_mat.shape[1] // head_size
    resid_in = tokens.astype(f32)
    r_one = lax.rsqrt(jnp.mean(resid_in * resid_in, axis=-1, keepdims=True) + eps)
    attn_in = rms_apply(both_tokens.reshape(-1, width).astype(f32), gain_pa)[0].astype(bf16)
    row_count = attn_in.shape[0]
    segment_row = segment_ids[0]
    position = positions_of(segment_row)
    allowed = build_allowed(segment_row)
    query_raw = jnp.dot(attn_in, query_mat, preferred_element_type=f32).reshape(
        row_count, heads_local, head_size
    )
    key_raw = jnp.dot(attn_in, key_mat, preferred_element_type=f32)
    value_vec = jnp.dot(attn_in, value_mat, preferred_element_type=f32).astype(bf16)
    query_norm, r_query = rms_apply(query_raw, gain_q)
    key_norm, r_key = rms_apply(key_raw, gain_k)
    cosine_table, sine_table = rope_tables(position, head_size)
    query_rot = (
        query_norm * cosine_table[:, None, :] + rotate_half(query_norm) * sine_table[:, None, :]
    ).astype(bf16)
    key_rot = (key_norm * cosine_table + rotate_half(key_norm) * sine_table).astype(bf16)
    score_scale = head_size ** (-0.5)
    scores = jnp.einsum("qhd,kd->hqk", query_rot, key_rot, preferred_element_type=f32) * score_scale
    scores = jnp.where(allowed[None], scores, -jnp.inf)
    row_max = jnp.max(scores, axis=-1, keepdims=True)
    row_total = jnp.sum(jnp.exp(scores - row_max), axis=-1, keepdims=True)
    log_total = row_max + jnp.log(row_total)
    weights_full = jnp.where(allowed[None], jnp.exp(scores - log_total), 0.0)
    probs = weights_full.astype(bf16)
    context = (
        jnp.einsum("hqk,kd->qhd", probs, value_vec, preferred_element_type=f32)
        .astype(bf16)
        .reshape(row_count, heads_local * head_size)
    )
    attn_part = jnp.einsum("te,de->td", context, out_mat, preferred_element_type=f32)
    attn_raw = pair_call(attn_part, True, 4)
    attn_normed, r_two = rms_apply(attn_raw, gain_po)
    residual = resid_in + attn_normed
    ffn_local, r_three = rms_apply(residual, gain_pf)
    output, d_ffn_input, grad_gpp, ffn_grads = ffn_all(
        ffn_local.astype(bf16), residual, cotangent, gain_pp[None], buf
    )
    grad_out = cotangent.astype(f32)
    d_resid_norm, grad_gpf = rms_back(residual, r_three, gain_pf, d_ffn_input)
    d_residual = grad_out + d_resid_norm
    d_attn_local, grad_gpo = rms_back(attn_raw, r_two, gain_po, d_residual)
    d_attn_raw = pair_call(d_attn_local.astype(bf16), False, 5)
    d_context = jnp.dot(d_attn_raw, out_mat, preferred_element_type=f32).astype(bf16)
    grad_out_mat = jnp.einsum("td,te->de", d_attn_raw, context, preferred_element_type=f32)
    d_context = d_context.reshape(row_count, heads_local, head_size)
    d_prob = jnp.einsum("qhd,kd->hqk", d_context, value_vec, preferred_element_type=f32)
    delta = jnp.sum(weights_full * d_prob, axis=-1, keepdims=True)
    d_score = (weights_full * (d_prob - delta) * score_scale).astype(bf16)
    d_query_rot = jnp.einsum("hqk,kd->qhd", d_score, key_rot, preferred_element_type=f32)
    d_query_norm = d_query_rot * cosine_table[:, None, :] - rotate_half(
        d_query_rot * sine_table[:, None, :]
    )
    d_query, grad_gq = rms_back(query_raw, r_query, gain_q, d_query_norm)
    d_query = d_query.astype(bf16).reshape(row_count, heads_local * head_size)
    d_key_rot = jnp.einsum("hqk,qhd->kd", d_score, query_rot, preferred_element_type=f32)
    d_key_norm = d_key_rot * cosine_table - rotate_half(d_key_rot * sine_table)
    d_key, grad_gk = rms_back(key_raw, r_key, gain_k, d_key_norm)
    d_key = d_key.astype(bf16)
    d_value = jnp.einsum("hqk,qhd->kd", probs, d_context, preferred_element_type=f32).astype(bf16)
    d_in_part = jnp.einsum("te,de->td", d_query, query_mat, preferred_element_type=f32)
    d_in_part = d_in_part + jnp.einsum("te,de->td", d_key, key_mat, preferred_element_type=f32)
    d_in_part = d_in_part + jnp.einsum("te,de->td", d_value, value_mat, preferred_element_type=f32)
    d_attn_in = pair_call(d_in_part, True, 6)
    grad_query = jnp.einsum("td,te->de", attn_in, d_query, preferred_element_type=f32)
    grad_key = jnp.einsum("td,te->de", attn_in, d_key, preferred_element_type=f32)
    grad_value = jnp.einsum("td,te->de", attn_in, d_value, preferred_element_type=f32)
    d_input_norm, grad_gpa = rms_back(resid_in, r_one, gain_pa, d_attn_in)
    grad_tokens = d_residual + d_input_norm

    def blocks(grad):
        return jnp.moveaxis(grad.astype(bf16).reshape(width, -1, 128), 1, 0)

    one = jnp.concatenate([blocks(grad_query), blocks(grad_key)])
    two = jnp.concatenate([blocks(grad_value), blocks(grad_out_mat)])
    shape = (6, 2, 4, ROWS, 128)
    attn_own = jnp.where(core == 0, one, two).reshape(shape)
    attn_other = jnp.where(core == 0, two, one).reshape(shape)
    small = [g.reshape(64, 18) for g in (grad_gpa, grad_gpo, grad_gpf, grad_gpp)]
    small += [g.reshape(64, 4) for g in (grad_gq, grad_gk)]
    small = jnp.pad(jnp.concatenate(small, axis=1), ((0, 0), (0, 48))).reshape(2, 4, 8, 128)
    sums = scatter_all(attn_own, attn_other, ffn_grads.reshape(42, 2, 4, ROWS, 128), small)
    s_query, s_key, s_value, s_out, s_gate, s_up, s_down, s_gains = sums
    s_gains = lax.dynamic_index_in_dim(s_gains, lax.rem(my_dp, 8), 0, keepdims=False)
    s_pa, s_po, s_pf, s_pp = [s_gains[18 * n : 18 * n + 18] for n in range(4)]
    return (
        output, grad_tokens, s_query, s_key, s_value, s_out, s_gains[72:76], s_gains[76:80],
        s_pa, s_po, s_gate, s_up, s_down, s_pf, s_pp,
    )


def solution(mesh):
    return jax.shard_map(
        local,
        mesh=mesh,
        in_specs=(
            P(("dp", "tensor"), None),
            P("dp", None),
            P("dp", "tensor"),
            P("dp", None),
            P("dp", None),
            P("dp", "tensor"),
            P("dp"),
            P("dp"),
            P("dp"),
            P("dp"),
            P("dp", "tensor"),
            P("dp", "tensor"),
            P("dp", "tensor"),
            P("dp"),
            P("dp"),
            P(("dp", "tensor"), None),
        ),
        out_specs=(
            P(("dp", "tensor"), None),
            P(("dp", "tensor"), None),
            P("dp", "tensor"),
            P("dp", None),
            P("dp", None),
            P("dp", "tensor"),
            P("dp"),
            P("dp"),
            P("dp"),
            P("dp"),
            P("dp", "tensor"),
            P("dp", "tensor"),
            P("dp", "tensor"),
            P("dp"),
            P("dp"),
        ),
        check_vma=False,
    )
```

time: 1300 us -> 402 us (0.31)
  waiting for transfers between devices: 641 us -> 0 us
  Pallas kernels: 0 us -> 308 us
  blocking collectives: 207 us -> 0 us
  starting transfers between devices: 164 us -> 0 us
  local copies, waits for them, and re-layouts: 128 us -> 41.9 us
  matrix products: 79 us -> 16.5 us
  other arithmetic: 57.4 us -> 27.5 us
  between operations: 17.7 us -> 2.13 us
    all_to_all x20 -> x0, waiting for transfers between devices: 516 us -> none  [the longest x1 147 us: local(): lax.all_to_all(split_rows(every_term[8], shard_count).astype(jnp.bfloat16...]
    pallas_call x0 -> x6, Pallas kernels: none -> 308 us  [the longest x1 99.5 us: scatter_all(): pl.pallas_call(scatter_kernel, name='scatter_grads', out_shape=tuple((jax...]
    all_to_all x20 -> x0, starting transfers between devices: 164 us -> none  [the longest x1 20.3 us: local(): lax.all_to_all(split_rows(every_term[12], shard_count).astype(jnp.bfloat1...]
    all_gather x2 -> x0, waiting for transfers between devices: 125 us -> none  [the longest x1 125 us: sent_together(): result = lax.all_gather(both, axis, axis=dim, tiled=True)]
    unnamed x1 -> x0, blocking collectives: 112 us -> none
    all_to_all x9 -> x0, blocking collectives: 94.8 us -> none  [the longest x7 60.8 us: copy_for_each(): return lax.all_to_all(copies, axis, split_axis=0, concat_axis=0, tiled=True)]
    dot_general x9 -> x0, matrix products: 52.2 us -> none  [the longest x1 7.9 us: local(): d_hidden = jnp.dot(d_ffn_raw, down_mat, preferred_element_type=f32)]
    convert_element_type x16 -> x0, local copies, waits for them, and re-layouts: 49.4 us -> none  [the longest x1 11.8 us: local(): split_rows(every_term[9], shard_count).astype(jnp.bfloat16)]
  transfers between devices with their start and end apart: 22 -> 0, of which waited for: 18 -> 0; matrix products, arithmetic and copies ran while one was open for 13% -> 0% of each run, Pallas kernels for 0% -> 0%
where the time goes in v1:
time: 402 us; the launch traced here: 396 us
  Pallas kernels  308 us (77%)
  local copies, waits for them, and re-layouts  41.9 us (10%)
  other arithmetic  27.5 us (7%)
  matrix products  16.5 us (4%)
    pallas_call x1, Pallas kernels, scatter_all(): pl.pallas_call(scatter_kernel, name='scatter_grads', out_shape=tuple((jax...  99.5 us
    pallas_call x1, Pallas kernels, gather_all(): pl.pallas_call(gather_kernel, name='gather_weights', out_shape=(jax.Shape...  96.6 us
    pallas_call x1, Pallas kernels, ffn_all(): pl.pallas_call(ffn_kernel, name='ffn_layer', out_shape=(jax.ShapeDtypeStr...  80.7 us
    pallas_call x3, Pallas kernels, pair_call(): pl.pallas_call(functools.partial(pair_kernel, reduce), name='pair_sum' if...  30.8 us
    unnamed x112, local copies, waits for them, and re-layouts  17.2 us

profile of v1, /device:TPU:45, one launch (start us, length us, event | category | flops | bytes accessed | tf_op | source)
XLA Modules:
  0.0 395.6 jit_solution(13682326545135909589)
XLA Ops:
  2.5 4.1 %concatenate.47 = bf16[80]{0:T(256)(128)(2,1)S(1)} concatenate(bf16[18]{0:T(256)(128)(2,1)} %param.24, bf16[18]{0:T(256)(128)(2,1)} %param.25, bf16[18]{0:T(256)(128)(2,1)} %param.29, bf16[18]{0:T(256)(128)(2,1)} %param.30, bf16[4]{0:T(256)(128)(2,1)} %param.22, bf16[4]{0:T(256)(128)(2,1)} %param.23), dimensions={0} | concatenate | bytes 320 | tf_op jit(solution)/shard_map/concatenate | solution.py:833
  8.6 1.5 fusion.32
  10.1 1.2 multiply_cosine_fusion
  11.4 96.6 %gather_weights.1 = (bf16[4,12,2,4,144,128]{5,4,3,2,1,0:T(8,128)(2,1)}, bf16[6,2,4,144,128]{4,3,2,1,0:T(8,128)(2,1)}, f32[2,4,8,128]{3,2,1,0:T(8,128)}, bf16[2,128,1152]{2,1,0:T(8,128)(2,1)}) custom-call(bf16[18,512]{1,0:T(8,128)(2,1)} %q_ref.1, bf16[18,256]{1,0:T(8,128)(2,1)} %k_ref.1, bf16[18,256]{1,0:T(8,128)(2,1)} %v_ref.1, bf16[18,512]{1,0:T(8,128)(2,1)} %o_ref.1, ...), custom_call_target="tpu_custom_call" | custom-call | tf_op jit(solution)/shard_map/gather_weights/pallas_call | solution.py:329
  108.0 1.3 multiply_reduce_fusion
  114.3 1.8 bitcast_select_fusion
  119.1 1.8 copy.44
  125.0 1.7 copy.45
  130.7 1.6 fusion.56.src
  132.3 9.3 %pair_sum.2 = f32[128,1152]{1,0:T(8,128)} custom-call(f32[256,1152]{1,0:T(8,128)} %fusion.56.src), custom_call_target="tpu_custom_call" | custom-call | tf_op jit(solution)/shard_map/pair_sum/pallas_call | solution.py:646
  142.8 1.3 multiply_reduce_fusion.6
  145.6 80.7 %ffn_layer.1 = (bf16[128,1152]{1,0:T(8,128)(2,1)}, f32[128,1152]{1,0:T(8,128)}, f32[1,1152]{1,0:T(1,128)}, bf16[42,1152,128]{2,1,0:T(8,128)(2,1)}) custom-call(bf16[128,1152]{1,0:T(8,128)(2,1)} %multiply_convert_fusion.1.x_in, f32[128,1152]{1,0:T(8,128)} %copy-done, bf16[128,1152]{1,0:T(8,128)(2,1)} %cot.1, f32[1,1152]{1,0:T(1,128)} %broadcast_in_dim_reshape.3.gain, ...), custom_call_target="tpu_custom_call" | custom-call | tf_op jit(solution)/shard_map/ffn_layer/pallas_call | solution.py:778
  227.1 1.4 multiply_reduce_fusion.2
  228.5 1.6 multiply_reduce_fusion.3
  232.7 11.0 %pair_gather.1 = bf16[256,1152]{1,0:T(8,128)(2,1)} custom-call(bf16[128,1152]{1,0:T(8,128)(2,1)} %subtract_convert_fusion.src), custom_call_target="tpu_custom_call" | custom-call | tf_op jit(solution)/shard_map/pair_gather/pallas_call | solution.py:646
  243.8 1.7 convolution_convert_fusion.4
  248.6 1.7 broadcast_multiply_fusion
  255.3 1.4 convolution_add_fusion.src
  256.7 10.5 %pair_sum.3 = f32[128,1152]{1,0:T(8,128)} custom-call(f32[256,1152]{1,0:T(8,128)} %convolution_add_fusion.src), custom_call_target="tpu_custom_call" | custom-call | tf_op jit(solution)/shard_map/pair_sum/pallas_call | solution.py:646
  267.2 1.3 fusion.23
  272.4 1.5 convolution_convert_fusion
  273.9 1.7 copy.58
  275.7 1.2 convolution_convert_fusion.3
  278.1 1.4 copy.56
  279.4 2.1 copy.57
  281.6 3.1 broadcast_select_fusion
  284.7 99.5 %scatter_grads.1 = (f32[18,512]{1,0:T(8,128)}, f32[18,256]{1,0:T(8,128)}, f32[18,256]{1,0:T(8,128)}, f32[18,512]{1,0:T(8,128)}, f32[18,3456]{1,0:T(8,128)}, /*in...) custom-call(bf16[6,2,4,144,128]{4,3,2,1,0:T(8,128)(2,1)} %get-tuple-element.65.attn_own, ...), custom_call_target="tpu_custom_call" | custom-call | tf_op jit(solution)/shard_map/scatter_grads/pallas_call | solution.py:587
  386.9 1.4 copy.85
  388.3 1.3 copy.86
  389.6 1.3 copy.87
  391.0 1.4 copy.88
  392.4 1.7 copy.89
  (185 shorter events, 42.1 us)
Async XLA Ops:
  108.0 4.6 %copy-start.15 = (bf16[2,128,1152]{2,1,0:T(8,128)(2,1)S(1)}, bf16[2,128,1152]{2,1,0:T(8,128)(2,1)}, u32[]{:S(2)}) copy-start(bf16[2,128,1152]{2,1,0:T(8,128)(2,1)} %get-tuple-element.31) | copy-start | bytes 1769476
  112.6 1.7 copy-start.30
  113.8 12.9 %copy-start.3 = (bf16[2,128,1152]{2,1,0:T(8,128)(2,1)}, bf16[2,128,1152]{2,1,0:T(8,128)(2,1)S(1)}, u32[]{:S(2)}) copy-start(bf16[2,128,1152]{2,1,0:T(8,128)(2,1)S(1)} %multiply_convert_fusion) | copy-start | bytes 1769476
  119.1 10.9 %copy-start.18 = (bf16[1152,4,128]{0,2,1:T(8,128)(2,1)}, bf16[1152,4,128]{0,2,1:T(8,128)(2,1)S(1)}, u32[]{:S(2)}) copy-start(bf16[1152,4,128]{0,2,1:T(8,128)(2,1)S(1)} %copy.50) | copy-start | bytes 3538948
  121.3 1.5 copy-start.21
  122.9 4.9 %copy-start.24 = (f32[256,256]{0,1:T(8,128)}, f32[256,256]{0,1:T(8,128)S(1)}, u32[]{:S(2)}) copy-start(f32[256,256]{0,1:T(8,128)S(1)} %get-tuple-element.77) | copy-start | bytes 786436
  127.3 1.3 copy-start.5
  128.7 1.3 copy-start.45
  129.7 2.6 copy-start.49
  132.3 10.5 %copy-start.16 = (bf16[128,1152]{1,0:T(8,128)(2,1)S(1)}, bf16[128,1152]{1,0:T(8,128)(2,1)}, u32[]{:S(2)}) copy-start(bf16[128,1152]{1,0:T(8,128)(2,1)} %tok_ref.1) | copy-start | bytes 884740
  144.1 1.4 copy-start
  226.3 2.3 copy-start.1
  226.3 2.3 copy-start.2
  230.2 13.5 %copy-start.19 = (bf16[1152,4,128]{0,2,1:T(8,128)(2,1)S(1)}, bf16[1152,4,128]{0,2,1:T(8,128)(2,1)}, u32[]{:S(2)}) copy-start(bf16[1152,4,128]{0,2,1:T(8,128)(2,1)} %copy-done.18) | copy-start | bytes 3538948
  243.7 1.7 copy-start.29
  243.7 1.7 copy-start.44
  243.7 1.7 copy-start.50
  245.4 2.0 copy-start.39
  245.4 2.0 copy-start.46
  246.4 2.3 copy-start.25
  246.4 2.3 copy-start.37
  248.6 1.8 copy-start.33
  256.7 10.5 %copy-start.17 = (bf16[128,1152]{1,0:T(8,128)(2,1)S(1)}, bf16[128,1152]{1,0:T(8,128)(2,1)}, u32[]{:S(2)}) copy-start(bf16[128,1152]{1,0:T(8,128)(2,1)} %tok_ref.1) | copy-start | bytes 884740
  256.7 10.5 %copy-start.51 = (f32[128]{0:T(128)S(1)}, f32[128]{0:T(128)}, u32[]{:S(2)}) copy-start(f32[128]{0:T(128)} %add_rsqrt_fusion.3) | copy-start | bytes 1540
  267.2 1.4 copy-start.9
  268.5 1.4 copy-start.47
  268.5 1.5 copy-start.48
  268.6 2.2 copy-start.4
  273.9 1.8 copy-start.10
  284.7 101.5 %copy-start.42 = (bf16[128,1152]{1,0:T(8,128)(2,1)S(1)}, bf16[128,1152]{1,0:T(8,128)(2,1)}, u32[]{:S(2)}) copy-start(bf16[128,1152]{1,0:T(8,128)(2,1)} %get-tuple-element.123) | copy-start | bytes 884740
  384.2 9.9 %copy-start.41 = (f32[18,3456]{1,0:T(8,128)S(1)}, f32[18,3456]{1,0:T(8,128)}, u32[]{:S(2)}) copy-start(f32[18,3456]{1,0:T(8,128)} %get-tuple-element.134) | copy-start | bytes 746500
  384.2 10.7 %copy-start.40 = (f32[18,3456]{1,0:T(8,128)S(1)}, f32[18,3456]{1,0:T(8,128)}, u32[]{:S(2)}) copy-start(f32[18,3456]{1,0:T(8,128)} %get-tuple-element.135) | copy-start | bytes 746500
  (20 other events, 20.6 us)

commit v2 on v1

--- a/solution.py
+++ b/solution.py
@@ -11,20 +11,6 @@
 eps = 1e-06
 gelu_scale = 0.7978845608028654
 gelu_cube = 0.044715
-
-
-def rms_apply(values, gain_vec):
-    inverse = lax.rsqrt(jnp.mean(values * values, axis=-1, keepdims=True) + eps)
-    return (values * inverse * (1.0 + gain_vec), inverse)
-
-
-def rms_back(values, inverse, gain_vec, grad_out):
-    scaled = grad_out * (1.0 + gain_vec)
-    grad_value = inverse * scaled - values * inverse * inverse * inverse * jnp.mean(
-        scaled * values, axis=-1, keepdims=True
-    )
-    grad_gain = jnp.sum(grad_out * values * inverse, axis=tuple(range(values.ndim - 1)))
-    return (grad_value, grad_gain)
 
 
 def positions_of(segment_row):
@@ -52,11 +38,6 @@
     return (cosine_table, sine_table)
 
 
-def rotate_half(values):
-    half_width = values.shape[-1] // 2
-    return jnp.concatenate([-values[..., half_width:], values[..., :half_width]], axis=-1)
-
-
 f32 = jnp.float32
 bf16 = jnp.bfloat16
 MESH = pl.DeviceIdType.MESH
@@ -67,13 +48,25 @@
 VMEM_MOST = 66_000_000
 
 CLASSES = (
-    (0, 2, "zxy"),
-    (2, 4, "zyx"),
-    (4, 6, "xyz"),
-    (6, 8, "yxz"),
-    (8, 10, "zxy"),
-    (10, 12, "zyx"),
+    (0, 1, "zxy"),
+    (1, 2, "zyx"),
+    (2, 4, "zxy"),
+    (4, 6, "zyx"),
+    (6, 8, "zxy"),
+    (8, 10, "zyx"),
+    (10, 11, "xyz"),
+    (11, 12, "yxz"),
 )
+ATTN_CLASSES = (0, 1)
+ROW_CUT = 80
+
+
+def place(block):
+    return block // 10 * 12 + 2 + block % 10 if block < 30 else 6 + block
+
+
+def attn_place(block):
+    return block // 2 * 12 + block % 2
 
 
 def coords():
@@ -95,7 +88,15 @@
     attn = [("q", j) for j in range(4)] + [("k", j) for j in range(2)]
     attn_two = [("v", j) for j in range(2)] + [("o", j) for j in range(4)]
     ffn = [[(n, j) for n in "gud" for j in range(14)], [(n, j + 14) if j < 13 else None for n in "gud" for j in range(14)]]
-    return [attn + ffn[0], attn_two + ffn[1]]
+    cores = []
+    for small, large in ((attn, ffn[0]), (attn_two, ffn[1])):
+        spots = [None] * 48
+        for n, source in enumerate(small):
+            spots[attn_place(n)] = source
+        for n, source in enumerate(large):
+            spots[place(n)] = source
+        cores.append(spots)
+    return cores
 
 
 def enter(peers):
@@ -124,11 +125,22 @@
     return p["c"] * 4 + p["y"]
 
 
-def part_of(buf, at, done, dim, index, i0, i1):
+def part_of(buf, at, done, dim, index, i0, i1, side=None):
     pick = {d: (slice(None) if d in done else at[d]) for d in "zxy"}
     if dim is not None:
         pick[dim] = index
-    return buf.at[pick["y"], i0:i1, pick["z"], pick["x"]]
+    (lo, hi), rows = side_of(i0, i1, side)
+    return buf.at[pick["y"], lo:hi, pick["z"], pick["x"], rows[0] : rows[1]]
+
+
+def side_of(i0, i1, side):
+    n = i1 - i0
+    if side is None:
+        return (i0, i1), (0, ROWS)
+    if n % 2 == 0:
+        mid = i0 + n // 2
+        return ((i0, mid), (mid, i1))[side], (0, ROWS)
+    return (i0, i1), ((0, ROW_CUT), (ROW_CUT, ROWS))[side]
 
 
 def size_of(done, n):
@@ -138,16 +150,23 @@
     return size
 
 
-def order_gather(classes, rate=46e3, hop=1.6):
+def order_gather(classes, early, pieces, rate=46e3, hop=1.6):
     free, events, queue = {}, [], []
-    for k, (i0, i1, order) in enumerate(classes):
+    left = len(early)
+    for k in range(len(classes)):
         queue.append((0.0, k, 0, 0))
     while queue:
         queue.sort()
         ready, k, ph, st = queue.pop(0)
+        if k < 0:
+            events.append((ph,))
+            continue
         i0, i1, order = classes[k]
         events.append((k, ph, st))
         if ph == len(order):
+            left -= k in early
+            if k in early and not left:
+                queue += [(ready + t, -1, n, 0) for n, t in enumerate(pieces)]
             continue
         dim, done = order[ph], order[:ph]
         size = size_of(done, i1 - i0)
@@ -165,11 +184,110 @@
     return events
 
 
+def normed(values, gain):
+    inverse = lax.rsqrt(jnp.mean(values * values, axis=-1, keepdims=True) + eps)
+    return values * inverse * (1.0 + gain), inverse
+
+
+def norm_back(values, gain, grad):
+    inverse = lax.rsqrt(jnp.mean(values * values, axis=-1, keepdims=True) + eps)
+    scaled = grad * (1.0 + gain)
+    mean = jnp.mean(scaled * values, axis=-1, keepdims=True)
+    back = inverse * scaled - values * inverse * inverse * inverse * mean
+    return back, jnp.sum(grad * values * inverse, axis=0, keepdims=True)
+
+
+def half_turn(values):
+    return jnp.concatenate([-values[:, 128:], values[:, :128]], axis=1)
+
+
+def last_dot(a, b):
+    return lax.dot_general(a, b, (((1,), (1,)), ((), ())), preferred_element_type=f32)
+
+
+def spread_marks(each, offset, width):
+    lane = lax.broadcasted_iota(jnp.int32, (128, width), 0)
+    entry = lax.broadcasted_iota(jnp.int32, (128, width), 1)
+    picks = lane == offset + lax.rem(entry, each)
+    dev = lax.broadcasted_iota(jnp.int32, (64, width), 0)
+    owns = lax.div(lax.broadcasted_iota(jnp.int32, (64, width), 1), each) == dev
+    return picks, owns
+
+
+def spread_gains(gbuf, gain_d, gain_h):
+    tile = gbuf[...].reshape(64, 128).astype(bf16)
+    for n in range(4):
+        picks, owns = spread_marks(SHARD, SHARD * n, gain_d.shape[1])
+        wide = jnp.dot(tile, picks.astype(f32).astype(bf16), preferred_element_type=f32)
+        gain_d[n : n + 1, :] = jnp.sum(jnp.where(owns, wide, 0.0), axis=0, keepdims=True)
+    for n in range(2):
+        picks, owns = spread_marks(4, 4 * SHARD + 4 * n, 256)
+        wide = jnp.dot(tile, picks.astype(f32).astype(bf16), preferred_element_type=f32)
+        gain_h[n : n + 1, :] = jnp.sum(jnp.where(owns, wide, 0.0), axis=0, keepdims=True)
+
+
+def fold_gains(grads_d, grads_h):
+    total = jnp.zeros((64, 128), f32)
+    for n in range(4):
+        picks, owns = spread_marks(SHARD, SHARD * n, grads_d[n].shape[1])
+        wide = jnp.where(owns, grads_d[n], 0.0)
+        total += lax.dot_general(
+            wide, picks.astype(f32), (((1,), (1,)), ((), ())),
+            precision=lax.Precision.HIGHEST, preferred_element_type=f32,
+        )
+    for n in range(2):
+        picks, owns = spread_marks(4, 4 * SHARD + 4 * n, 256)
+        wide = jnp.where(owns, grads_h[n], 0.0)
+        total += lax.dot_general(
+            wide, picks.astype(f32), (((1,), (1,)), ((), ())),
+            precision=lax.Precision.HIGHEST, preferred_element_type=f32,
+        )
+    return total
+
+
+def blocks_of(w, first, count):
+    width = 8 * ROWS
+    return jnp.concatenate([w[first + n].reshape(width, 128) for n in range(count)], axis=1)
+
+
+def attn_forward(at, attn_in, w, cos, sin, allowed, q_raw, k_raw, value, q_rot, k_rot, soft, context, part, gain_h):
+    def queries():
+        q_raw[...] = jnp.dot(attn_in[...], blocks_of(w, 0, 4), preferred_element_type=f32)
+        for h in range(2):
+            lanes = slice(256 * h, 256 * h + 256)
+            q = normed(q_raw[:, lanes], gain_h[0:1, :])[0]
+            q_rot[:, lanes] = (q * cos[...] + half_turn(q) * sin[...]).astype(bf16)
+
+    def keys():
+        key = jnp.dot(attn_in[...], blocks_of(w, 4, 2), preferred_element_type=f32)
+        k_raw[...] = key
+        key = normed(key, gain_h[1:2, :])[0]
+        k_rot[...] = (key * cos[...] + half_turn(key) * sin[...]).astype(bf16)
+        value[...] = jnp.dot(attn_in[...], blocks_of(w, 6, 2), preferred_element_type=f32).astype(bf16)
+
+    def heads():
+        seen = allowed[...] > 0.0
+        for h in range(2):
+            lanes = slice(256 * h, 256 * h + 256)
+            scores = last_dot(q_rot[:, lanes], k_rot[...]) * (256.0 ** -0.5)
+            scores = jnp.where(seen, scores, -jnp.inf)
+            top = jnp.max(scores, axis=-1, keepdims=True)
+            total = jnp.sum(jnp.exp(scores - top), axis=-1, keepdims=True)
+            full = jnp.where(seen, jnp.exp(scores - (top + jnp.log(total))), 0.0)
+            soft[h] = full
+            context[:, lanes] = jnp.dot(full.astype(bf16), value[...], preferred_element_type=f32).astype(bf16)
+
+    def project():
+        part[...] = last_dot(context[...], blocks_of(w, 8, 4))
+
+    return [queries, keys, heads, project]
+
+
 def gather_kernel(
-    q_ref, k_ref, v_ref, o_ref, g_ref, u_ref, d_ref, gains_ref, tok_ref,
-    buf, other, gbuf, tok_out,
-    send, got, own32, own, ggot, gmine,
-    a_send, a_recv, g_send, g_recv, s_sem, r_sem, e_sem, l_sem,
+    q_ref, k_ref, v_ref, o_ref, g_ref, u_ref, d_ref, gains_ref, tok_ref, cos_ref, sin_ref, allowed_ref,
+    buf, other, attn_in, q_raw, k_raw, value, q_rot, k_rot, soft, context, attn_raw, residual, ffn_in, gain_d, gain_h,
+    send, got, own32, own, ggot, gmine, gbuf, tok_out, w, part, pstage, pland,
+    a_send, a_recv, g_send, g_recv, s_sem, r_sem, e_sem, l_sem, w_sem,
 ):
     at = coords()
     refs = {"q": q_ref, "k": k_ref, "v": v_ref, "o": o_ref, "g": g_ref, "u": u_ref, "d": d_ref}
@@ -231,7 +349,6 @@
     def incoming(k, ph, st):
         i0, i1, order = CLASSES[k]
         dim, done = order[ph], order[:ph]
-        half = (i1 - i0) // 2
         if dim == "z":
             return [(part_of(buf, at, done, "z", 1 - at["z"], i0, i1), r_sem.at[k, ph, 0])]
         left, right = ahead(at, dim, -1), ahead(at, dim, 1)
@@ -242,8 +359,8 @@
             ]
         across = ahead(at, dim, 2)
         return [
-            (part_of(buf, at, done, dim, across, i0, i0 + half), r_sem.at[k, ph, 2]),
-            (part_of(buf, at, done, dim, across, i0 + half, i1), r_sem.at[k, ph, 3]),
+            (part_of(buf, at, done, dim, across, i0, i1, 0), r_sem.at[k, ph, 2]),
+            (part_of(buf, at, done, dim, across, i0, i1, 1), r_sem.at[k, ph, 3]),
         ]
 
     def await_step(k, ph, st):
@@ -271,7 +388,67 @@
         ref = gbuf.at[z, x]
         remote(ref, ref, g_send.at[0], g_recv.at[8 + n], partner).wait_recv()
 
-    for k, ph, st in order_gather(CLASSES):
+    pair_copy = remote(pstage, pland, e_sem.at[4], e_sem.at[5], mirror)
+    swaps = [remote(buf.at[y, 0:2], other.at[y], e_sem.at[6 + y], e_sem.at[9 + y], partner) for y in range(3)]
+
+    def swap_start():
+        for copy in swaps:
+            copy.start()
+
+    def small_start():
+        glocal.wait()
+        gwait(ahead(at, "x", -1), at["z"], 0)
+        gwait(ahead(at, "x", 1), at["z"], 1)
+        fwd = gbuf.at[at["z"], ahead(at, "x", -1)]
+        gpush(fwd, fwd, 2, xr)
+
+    def small_next():
+        gwait(ahead(at, "x", 2), at["z"], 2)
+        gpush(gbuf.at[at["z"]], gbuf.at[at["z"]], 3, zo)
+
+    def attn_weights():
+        ref = gbuf.at[1 - at["z"]]
+        remote(ref, ref, g_send.at[0], g_recv.at[11], partner).wait_recv()
+        for copy in swaps:
+            copy.wait()
+        base = at["c"] * 6
+        copies = []
+        for y in range(3):
+            copies.append(pltpu.make_async_copy(buf.at[y, 0:2], w.at[pl.ds(base + 2 * y, 2)], w_sem.at[y]))
+            copies.append(pltpu.make_async_copy(other.at[y], w.at[pl.ds(6 - base + 2 * y, 2)], w_sem.at[3 + y]))
+        for copy in copies:
+            copy.start()
+        spread_gains(gbuf, gain_d, gain_h)
+        tok_local.wait()
+        ref = tok_out.at[1 - at["t"]]
+        remote(ref, ref, e_sem.at[2], e_sem.at[3], partner).wait_recv()
+        attn_in[...] = normed(tok_out[...].reshape(attn_in.shape).astype(f32), gain_d[0:1, :])[0].astype(bf16)
+        for copy in copies:
+            copy.wait()
+
+    pieces = [swap_start, small_start, small_next, attn_weights]
+    pieces += attn_forward(at, attn_in, w, cos_ref, sin_ref, allowed_ref, q_raw, k_raw, value, q_rot, k_rot, soft, context, part, gain_h)
+
+    def pair_start():
+        far = pl.ds(pl.multiple_of((1 - at["t"]) * 128, 128), 128)
+        pstage[...] = part[far, :].astype(bf16)
+        pair_copy.start()
+
+    def pair_end():
+        near = pl.ds(pl.multiple_of(at["t"] * 128, 128), 128)
+        pair_copy.wait()
+        raw = part[near, :] + pland[...].astype(f32)
+        attn_raw[...] = raw
+        res = tok_ref[...].astype(f32) + normed(raw, gain_d[1:2, :])[0]
+        residual[...] = res
+        ffn_in[...] = normed(res, gain_d[2:3, :])[0].astype(bf16)
+
+    pieces += [pair_start, pair_end]
+    for event in order_gather(CLASSES, ATTN_CLASSES, (0.0, 0.0, 3.0, 6.0, 9.0, 12.0, 15.0, 18.0, 20.0, 33.0)):
+        if len(event) == 1:
+            pieces[event[0]]()
+            continue
+        k, ph, st = event
         i0, i1, order = CLASSES[k]
         if st == 1:
             await_step(k, ph, 0)
@@ -280,7 +457,6 @@
         if ph == 3:
             continue
         dim, done = order[ph], order[:ph]
-        half = (i1 - i0) // 2
         if ph > 0 and not local_waited:
             local.wait()
             local_waited.append(1)
@@ -299,44 +475,46 @@
             push(mine_part(i0, i1), target, k, ph, 0, right)
             push(mine_part(i0, i1), target, k, ph, 1, left)
         else:
-            a = part_of(buf, at, done, dim, ahead(at, dim, -1), i0, i0 + half)
-            b = part_of(buf, at, done, dim, ahead(at, dim, 1), i0 + half, i1)
+            a = part_of(buf, at, done, dim, ahead(at, dim, -1), i0, i1, 0)
+            b = part_of(buf, at, done, dim, ahead(at, dim, 1), i0, i1, 1)
             push(a, a, k, ph, 2, right)
             push(b, b, k, ph, 3, left)
-    swap = remote(buf.at[0, 0:6], other, e_sem.at[0], e_sem.at[1], partner)
-    swap.start()
-    glocal.wait()
-    gwait(ahead(at, "x", -1), at["z"], 0)
-    gwait(ahead(at, "x", 1), at["z"], 1)
-    fwd = gbuf.at[at["z"], ahead(at, "x", -1)]
-    gpush(fwd, fwd, 2, xr)
-    gwait(ahead(at, "x", 2), at["z"], 2)
-    gpush(gbuf.at[at["z"]], gbuf.at[at["z"]], 3, zo)
-    ref = gbuf.at[1 - at["z"]]
-    remote(ref, ref, g_send.at[0], g_recv.at[11], partner).wait_recv()
     for copy in pending:
         copy.wait_send()
-    tok_local.wait()
     tok.wait_send()
-    ref = tok_out.at[1 - at["t"]]
-    remote(ref, ref, e_sem.at[2], e_sem.at[3], partner).wait_recv()
-    swap.wait()
-
-
-def gather_all(w, gains, tokens):
+
+
+def gather_all(w, gains, tokens, cos, sin, allowed):
     n = len(CLASSES)
     dma = pltpu.SemaphoreType.DMA
+    half, width = tokens.shape
+    rows = 2 * half
+
+    def shape(*dims, kind=f32):
+        return jax.ShapeDtypeStruct(dims, kind)
+
     return pl.pallas_call(
         gather_kernel,
-        name="gather_weights",
+        name="gather_and_attend",
         out_shape=(
-            jax.ShapeDtypeStruct((4, 12, 2, 4, ROWS, 128), bf16),
-            jax.ShapeDtypeStruct((6, 2, 4, ROWS, 128), bf16),
-            jax.ShapeDtypeStruct((2, 4, 8, 128), f32),
-            jax.ShapeDtypeStruct((2, *tokens.shape), bf16),
+            shape(4, 12, 2, 4, ROWS, 128, kind=bf16),
+            shape(3, 2, 2, 4, ROWS, 128, kind=bf16),
+            shape(rows, width, kind=bf16),
+            shape(rows, 512),
+            shape(rows, 256),
+            shape(rows, 256, kind=bf16),
+            shape(rows, 512, kind=bf16),
+            shape(rows, 256, kind=bf16),
+            shape(2, rows, rows),
+            shape(rows, 512, kind=bf16),
+            shape(half, width),
+            shape(half, width),
+            shape(half, width, kind=bf16),
+            shape(4, width),
+            shape(2, 256),
         ),
-        in_specs=[VMEM_SPEC] * 9,
-        out_specs=[ANY_SPEC] * 4,
+        in_specs=[VMEM_SPEC] * 12,
+        out_specs=[ANY_SPEC] * 2 + [VMEM_SPEC] * 13,
         scratch_shapes=[
             pltpu.VMEM((8, 12, SHARD, 128), bf16),
             pltpu.VMEM((8, 12, SHARD, 128), bf16),
@@ -344,26 +522,37 @@
             pltpu.VMEM((12, ROWS, 128), bf16),
             pltpu.VMEM((8, 8, 128), f32),
             pltpu.VMEM((8, 128), f32),
+            pltpu.VMEM((2, 4, 8, 128), f32),
+            pltpu.VMEM((2, half, width), bf16),
+            pltpu.VMEM((12, 2, 4, ROWS, 128), bf16),
+            pltpu.VMEM((rows, width), f32),
+            pltpu.VMEM((half, width), bf16),
+            pltpu.VMEM((half, width), bf16),
             dma((8,)),
             dma((8,)),
             dma((12,)),
             dma((12,)),
             dma((n, 3, 4)),
             dma((n, 3, 4)),
-            dma((4,)),
+            dma((12,)),
             dma((3,)),
+            dma((6,)),
         ],
         compiler_params=pltpu.CompilerParams(collective_id=1, has_side_effects=True, vmem_limit_bytes=VMEM_MOST),
-    )(*w, gains, tokens)
-
-
-def order_scatter(classes, rate=46e3, hop=2.5):
+    )(*w, gains, tokens, cos, sin, allowed)
+
+
+def order_scatter(classes, late, pieces, begin, rate=46e3, hop=2.5):
     free, events, queue = {}, [], []
     for k in range(len(classes)):
-        queue.append((0.0, k, 0, 0))
+        queue.append((begin if k in late else 0.0, k, 0, 0))
+    queue += [(t, -1, n, 0) for n, t in enumerate(pieces)]
     while queue:
         queue.sort()
         ready, k, ph, st = queue.pop(0)
+        if k < 0:
+            events.append((ph,))
+            continue
         i0, i1, order = classes[k]
         events.append((k, ph, st))
         if ph == len(order):
@@ -371,79 +560,100 @@
         dim, done = order[2 - ph], order[: 2 - ph]
         size = size_of(done, i1 - i0)
         if dim == "z":
-            ways, moved, follow = ("z+",), size, (k, ph + 1, 0)
+            ways, moved, waited, follow = ("z+",), size, size, (k, ph + 1, 0)
         elif st == 0:
-            ways, moved, follow = (dim + "+", dim + "-"), size / 2, (k, ph, 1)
+            ways, moved, waited, follow = (dim + "+", dim + "-"), size, size / 2, (k, ph, 1)
         else:
-            ways, moved, follow = (dim + "+", dim + "-"), size, (k, ph + 1, 0)
+            ways, moved, waited, follow = (dim + "+", dim + "-"), size / 2, size / 2, (k, ph + 1, 0)
         end = 0.0
         for way in ways:
-            begin = max(ready, free.get(way, 0.0))
-            free[way] = begin + (size if dim != "z" and st == 0 else moved if dim == "z" else size / 2) / rate
-            end = max(end, begin + (moved if st == 0 else size / 2) / rate)
+            first = max(ready, free.get(way, 0.0))
+            free[way] = first + moved / rate
+            end = max(end, first + waited / rate)
         queue.append((end + hop, *follow))
     return events
 
 
-def recv_shape(done, n):
-    return (*((4,) if "y" in done else ()), n, *((2,) if "z" in done else ()), *((4,) if "x" in done else ()), ROWS, 128)
+def recv_shape(done, n, rows):
+    return (*((4,) if "y" in done else ()), n, *((2,) if "z" in done else ()), *((4,) if "x" in done else ()), rows, 128)
 
 
 def scatter_shapes():
     shapes = []
     for i0, i1, order in CLASSES:
-        n = i1 - i0
         for ph in range(3):
             dim, done = order[2 - ph], order[: 2 - ph]
-            if dim == "z":
-                shapes.append(recv_shape(done, n))
-            else:
-                shapes.append((4, *recv_shape(done, n // 2)))
-                shapes.append((2, *recv_shape(done, n // 2)))
+            for side in (None,) if dim == "z" else (0, 1):
+                (lo, hi), rows = side_of(i0, i1, side)
+                one = recv_shape(done, hi - lo, rows[1] - rows[0])
+                shapes.append(one if side is None else (3, *one))
     return shapes
 
 
-def add_into(acc_part, refs):
-    shape = acc_part.shape[:-2]
-    total = math.prod(shape)
-
-    @pl.loop(0, total)
-    def _(at):
-        index, rest = [], at
+def combine(target, refs):
+    shape = target.shape[:-2]
+
+    @pl.loop(0, math.prod(shape))
+    def _(n):
+        index, rest = [], n
         for size in reversed(shape):
             index.insert(0, lax.rem(rest, size))
             rest = rest // size
-        value = acc_part[tuple(index)].astype(f32)
-        for ref in refs:
+        value = refs[0][tuple(index)].astype(f32)
+        for ref in refs[1:]:
             value = value + ref[tuple(index)].astype(f32)
-        acc_part[tuple(index)] = value.astype(bf16)
+        target[tuple(index)] = value.astype(bf16)
+
+
+def add_into(target, refs):
+    combine(target, [target, *refs])
+
+
+def rope_back(grad, cos, sin):
+    return grad * cos - half_turn(grad * sin)
 
 
 def scatter_kernel(
-    attn_own, attn_other, ffn, gains,
-    q_out, k_out, v_out, o_out, g_out, u_out, d_out, gains_out,
-    acc, pair, own32, send, got, gacc, grecv, ggot, kv, kvr, gfin, gfinal, gother, *rest,
+    ffn, buf, other, attn_in, q_raw, k_raw, value, q_rot, k_rot, soft, context, attn_raw, residual,
+    d_ffn, cot, tok, gain_d, gain_h, gpp, cos, sin,
+    q_out, k_out, v_out, o_out, g_out, u_out, d_out, gains_out, tok_out,
+    acc, pair, own32, send, got, gacc, grecv, ggot, kv, kvr, gfin, gfinal, gother,
+    w, ag, dfull, dctx, dq, dk, dv, part, pstage, pland, gsmall, gheads, *rest,
 ):
-    lands, (s_sem, r_sem, a_send, a_recv, g_send, g_recv, e_sem, l_sem) = rest[:-8], rest[-8:]
+    lands = rest[:-10]
+    s_sem, r_sem, a_send, a_recv, g_send, g_recv, e_sem, l_sem, f_sem, w_sem = rest[-10:]
     at = coords()
     group = group_peers(at)
     partner = device(at, c=1 - at["c"])
     mirror = device(at, t=1 - at["t"])
     ring = [device(at, x=ahead(at, "x", 1)), device(at, x=ahead(at, "x", -1)), device(at, z=1 - at["z"])]
     ring.append(device(at, x=ahead(at, "x", 2)))
-    loads = []
-    for y in range(4):
-        if y == 0:
-            loads.append(pltpu.make_async_copy(attn_own, acc.at[0, 0:6], l_sem.at[0]))
-            loads.append(pltpu.make_async_copy(ffn.at[0:6], acc.at[0, 6:12], l_sem.at[1]))
-        else:
-            loads.append(pltpu.make_async_copy(ffn.at[12 * y - 6 : 12 * y + 6], acc.at[y], l_sem.at[y + 1]))
-    loads.append(pltpu.make_async_copy(gains, gacc, l_sem.at[5]))
-    for copy in loads:
+    loads = {}
+    for k, (i0, i1, order) in enumerate(CLASSES):
+        loads[k] = []
+        for y in range(4):
+            if y == 3 or k not in ATTN_CLASSES:
+                b = 30 + i0 if y == 3 else 10 * y + i0 - 2
+                loads[k].append(pltpu.make_async_copy(ffn.at[b : b + i1 - i0], acc.at[y, i0:i1], f_sem.at[k, y]))
+    for k in (*range(2, len(CLASSES)), 0, 1):
+        for copy in loads[k]:
+            copy.start()
+    near = pl.ds(pl.multiple_of(at["t"] * 128, 128), 128)
+    far = pl.ds(pl.multiple_of((1 - at["t"]) * 128, 128), 128)
+    back, gsmall[2:3, :] = norm_back(residual[...], gain_d[2:3, :], d_ffn[...])
+    d_res = cot[...].astype(f32) + back
+    tok_out[...] = d_res
+    back, gsmall[1:2, :] = norm_back(attn_raw[...], gain_d[1:2, :], d_res)
+    dfull[near, :] = back.astype(bf16)
+    gsmall[3:4, :] = gpp[...]
+    base = at["c"] * 6
+    wloads = []
+    for y in range(3):
+        wloads.append(pltpu.make_async_copy(buf.at[y, 0:2], w.at[pl.ds(base + 2 * y, 2)], w_sem.at[y]))
+        wloads.append(pltpu.make_async_copy(other.at[y], w.at[pl.ds(6 - base + 2 * y, 2)], w_sem.at[3 + y]))
+    for copy in wloads:
         copy.start()
     enter([device(p) for p in group] + ring + [mirror])
-    swap = remote(attn_other, pair, e_sem.at[0], e_sem.at[1], partner)
-    swap.start()
     pending = []
 
     def push(src, dst, send_sem, recv_sem, to):
@@ -451,30 +661,106 @@
         copy.start()
         pending.append(copy)
 
-    for copy in loads:
-        copy.wait()
-    swap.wait()
-    add_into(acc.at[0, 0:6], [pair])
+    def await_ref(ref, sem):
+        remote(ref, ref, s_sem.at[0, 0, 0], sem, partner).wait_recv()
 
     zo = device(at, z=1 - at["z"])
-    push(gacc.at[1 - at["z"]], grecv.at[0:4], g_send.at[8], g_recv.at[8], zo)
-
+    push(dfull.at[near, :], dfull.at[near, :], e_sem.at[6], e_sem.at[7], mirror)
+    swap = remote(ag.at[pl.ds(6 - base, 6)], pair, e_sem.at[0], e_sem.at[1], partner)
+    pair_copy = remote(pstage, pland, e_sem.at[8], e_sem.at[9], mirror)
+
+    def to_blocks(grad, first):
+        grad = grad.astype(bf16)
+        for n in range(grad.shape[1] // 128):
+            ag[first + n] = grad[:, 128 * n : 128 * n + 128].reshape(2, 4, ROWS, 128)
+
+    def contexts():
+        await_ref(dfull.at[far, :], e_sem.at[7])
+        for copy in wloads:
+            copy.wait()
+        dctx[...] = jnp.dot(dfull[...], blocks_of(w, 8, 4), preferred_element_type=f32).astype(bf16)
+
+    def heads():
+        dk_rot = jnp.zeros((256, 256), f32)
+        d_value = jnp.zeros((256, 256), f32)
+        gq = jnp.zeros((1, 256), f32)
+        for h in range(2):
+            lanes = slice(256 * h, 256 * h + 256)
+            d_prob = last_dot(dctx[:, lanes], value[...])
+            full = soft[h]
+            delta = jnp.sum(full * d_prob, axis=-1, keepdims=True)
+            d_score = full * (d_prob - delta) * (256.0 ** -0.5)
+            score_b = d_score.astype(bf16)
+            dq_norm = rope_back(jnp.dot(score_b, k_rot[...], preferred_element_type=f32), cos[...], sin[...])
+            back, gain_part = norm_back(q_raw[:, lanes], gain_h[0:1, :], dq_norm)
+            dq[:, lanes] = back.astype(bf16)
+            gq = gq + gain_part
+            dk_rot = dk_rot + jnp.dot(score_b.T, q_rot[:, lanes], preferred_element_type=f32)
+            d_value = d_value + jnp.dot(full.astype(bf16).T, dctx[:, lanes], preferred_element_type=f32)
+        back, gk = norm_back(k_raw[...], gain_h[1:2, :], rope_back(dk_rot, cos[...], sin[...]))
+        dk[...] = back.astype(bf16)
+        dv[...] = d_value.astype(bf16)
+        gheads[0:1, :] = gq
+        gheads[1:2, :] = gk
+
+    def inputs():
+        part[...] = (
+            last_dot(dq[...], blocks_of(w, 0, 4))
+            + last_dot(dk[...], blocks_of(w, 4, 2))
+            + last_dot(dv[...], blocks_of(w, 6, 2))
+        )
+        pstage[...] = part[far, :].astype(bf16)
+        pair_copy.start()
+
+    def weight_grads():
+        left = attn_in[...].T
+        to_blocks(jnp.dot(left, dq[...], preferred_element_type=f32), 0)
+        to_blocks(jnp.dot(left, dk[...], preferred_element_type=f32), 4)
+        to_blocks(jnp.dot(left, dv[...], preferred_element_type=f32), 6)
+
+    def out_grads():
+        to_blocks(jnp.dot(dfull[...].T, context[...], preferred_element_type=f32), 8)
+        swap.start()
+
+    def finish():
+        pair_copy.wait()
+        d_in = part[near, :] + pland[...].astype(f32)
+        back, gsmall[0:1, :] = norm_back(tok[...].astype(f32), gain_d[0:1, :], d_in)
+        tok_out[...] = tok_out[...] + back
+        folded = fold_gains([gsmall[n : n + 1, :] for n in range(4)], [gheads[n : n + 1, :] for n in range(2)])
+        gacc[...] = folded.reshape(2, 4, 8, 128)
+        push(gacc.at[1 - at["z"]], grecv.at[0:4], g_send.at[8], g_recv.at[8], zo)
+
+    def merge():
+        swap.wait()
+        for y in range(3):
+            combine(acc.at[y, 0:2], [ag.at[pl.ds(base + 2 * y, 2)], pair.at[2 * y : 2 * y + 2]])
+
+    def small_x():
+        await_ref(grecv.at[0:4], g_recv.at[8])
+        gacc[at["z"]] = gacc[at["z"]] + grecv[0:4]
+        for n in range(1, 4):
+            xx = ahead(at, "x", n)
+            push(gacc.at[at["z"], xx], grecv.at[4 + n], g_send.at[8 + n], g_recv.at[8 + n], device(at, x=xx))
+
+    pieces = [contexts, heads, weight_grads, out_grads, inputs, merge, finish, small_x]
+    times = (11.0, 14.0, 18.0, 21.0, 23.0, 26.0, 37.0, 41.0)
     slots, position = {}, 0
     for k, (i0, i1, order) in enumerate(CLASSES):
         for ph in range(3):
-            if order[2 - ph] == "z":
-                slots[k, ph] = (lands[position],)
-                position += 1
-            else:
-                slots[k, ph] = (lands[position], lands[position + 1])
-                position += 2
-
-    def await_ref(ref, sem):
-        remote(ref, ref, s_sem.at[0, 0, 0], sem, partner).wait_recv()
-
-    for k, ph, st in order_scatter(CLASSES):
+            count = 1 if order[2 - ph] == "z" else 2
+            slots[k, ph] = lands[position : position + count]
+            position += count
+
+    for event in order_scatter(CLASSES, ATTN_CLASSES, times, 26.1):
+        if len(event) == 1:
+            pieces[event[0]]()
+            continue
+        k, ph, st = event
         i0, i1, order = CLASSES[k]
-        half = (i1 - i0) // 2
+        if st == 0 and ph == 0:
+            for copy in loads[k]:
+                copy.wait()
         if st == 0 and ph > 0:
             dim, done = order[3 - ph], order[: 3 - ph]
             if dim == "z":
@@ -482,11 +768,10 @@
                 await_ref(land, r_sem.at[k, ph - 1, 0])
                 add_into(part_of(acc, at, done, "z", at["z"], i0, i1), [land])
             else:
-                wide, _ = slots[k, ph - 1]
-                for n in range(4):
-                    await_ref(wide.at[n], r_sem.at[k, ph - 1, 2 + n])
-                add_into(part_of(acc, at, done, dim, at[dim], i0, i0 + half), [wide.at[0], wide.at[2]])
-                add_into(part_of(acc, at, done, dim, at[dim], i0 + half, i1), [wide.at[1], wide.at[3]])
+                for side, land in enumerate(slots[k, ph - 1]):
+                    await_ref(land.at[1], r_sem.at[k, ph - 1, 3 * side + 1])
+                    await_ref(land.at[2], r_sem.at[k, ph - 1, 3 * side + 2])
+                    add_into(part_of(acc, at, done, dim, at[dim], i0, i1, side), [land.at[1], land.at[2]])
         if ph == 3:
             continue
         dim, done = order[2 - ph], order[: 2 - ph]
@@ -495,31 +780,25 @@
             push(part_of(acc, at, done, "z", 1 - at["z"], i0, i1), land, s_sem.at[k, ph, 0], r_sem.at[k, ph, 0], zo)
             continue
         right, left = device(at, **{dim: ahead(at, dim, 1)}), device(at, **{dim: ahead(at, dim, -1)})
-        wide, narrow = slots[k, ph]
+        low, high = slots[k, ph]
         p1, m1, p2 = ahead(at, dim, 1), ahead(at, dim, -1), ahead(at, dim, 2)
-        lo, hi = (i0, i0 + half), (i0 + half, i1)
-
-        def sem(n):
-            return s_sem.at[k, ph, n], r_sem.at[k, ph, n]
+
+        def move(index, side, n, to):
+            src = part_of(acc, at, done, dim, index, i0, i1, side)
+            push(src, slots[k, ph][side].at[n], s_sem.at[k, ph, 3 * side + n], r_sem.at[k, ph, 3 * side + n], to)
 
         if st == 0:
-            push(part_of(acc, at, done, dim, p2, *lo), narrow.at[0], *sem(0), right)
-            push(part_of(acc, at, done, dim, p2, *hi), narrow.at[1], *sem(1), left)
-            push(part_of(acc, at, done, dim, p1, *hi), wide.at[1], *sem(3), right)
-            push(part_of(acc, at, done, dim, m1, *lo), wide.at[2], *sem(4), left)
+            move(p2, 0, 0, right)
+            move(p2, 1, 0, left)
+            move(p1, 1, 1, right)
+            move(m1, 0, 2, left)
         else:
-            await_ref(narrow.at[0], r_sem.at[k, ph, 0])
-            add_into(part_of(acc, at, done, dim, p1, *lo), [narrow.at[0]])
-            push(part_of(acc, at, done, dim, p1, *lo), wide.at[0], *sem(2), right)
-            await_ref(narrow.at[1], r_sem.at[k, ph, 1])
-            add_into(part_of(acc, at, done, dim, m1, *hi), [narrow.at[1]])
-            push(part_of(acc, at, done, dim, m1, *hi), wide.at[3], *sem(5), left)
-
-    await_ref(grecv.at[0:4], g_recv.at[8])
-    gacc[at["z"]] = gacc[at["z"]] + grecv[0:4]
-    for n in range(1, 4):
-        xx = ahead(at, "x", n)
-        push(gacc.at[at["z"], xx], grecv.at[4 + n], g_send.at[8 + n], g_recv.at[8 + n], device(at, x=xx))
+            await_ref(low.at[0], r_sem.at[k, ph, 0])
+            add_into(part_of(acc, at, done, dim, p1, i0, i1, 0), [low.at[0]])
+            move(p1, 0, 1, right)
+            await_ref(high.at[0], r_sem.at[k, ph, 3])
+            add_into(part_of(acc, at, done, dim, m1, i0, i1, 1), [high.at[0]])
+            move(m1, 1, 2, left)
 
     mine = at["y"] * 2 + at["c"]
     me = slot_of(at)
@@ -580,16 +859,18 @@
         copy.wait_send()
 
 
-def scatter_all(attn_own, attn_other, ffn, gains):
+def scatter_all(*operands):
     n = len(CLASSES)
     dma = pltpu.SemaphoreType.DMA
     widths = (512, 256, 256, 512, 3456, 3456, 3456)
+    out = [jax.ShapeDtypeStruct((SHARD, w), f32) for w in widths]
+    out += [jax.ShapeDtypeStruct((8, 128), f32), jax.ShapeDtypeStruct((128, 8 * ROWS), f32)]
     return pl.pallas_call(
         scatter_kernel,
-        name="scatter_grads",
-        out_shape=tuple(jax.ShapeDtypeStruct((SHARD, w), f32) for w in widths) + (jax.ShapeDtypeStruct((8, 128), f32),),
-        in_specs=[ANY_SPEC] * 4,
-        out_specs=[VMEM_SPEC] * 8,
+        name="attend_back_and_scatter",
+        out_shape=tuple(out),
+        in_specs=[ANY_SPEC] * 3 + [VMEM_SPEC] * 18,
+        out_specs=[VMEM_SPEC] * 9,
         scratch_shapes=[
             pltpu.VMEM((4, 12, 2, 4, ROWS, 128), bf16),
             pltpu.VMEM((6, 2, 4, ROWS, 128), bf16),
@@ -604,6 +885,18 @@
             pltpu.VMEM((8, 128), f32),
             pltpu.VMEM((8, 128), f32),
             pltpu.VMEM((8, 128), f32),
+            pltpu.VMEM((12, 2, 4, ROWS, 128), bf16),
+            pltpu.VMEM((12, 2, 4, ROWS, 128), bf16),
+            pltpu.VMEM((256, 8 * ROWS), bf16),
+            pltpu.VMEM((256, 512), bf16),
+            pltpu.VMEM((256, 512), bf16),
+            pltpu.VMEM((256, 256), bf16),
+            pltpu.VMEM((256, 256), bf16),
+            pltpu.VMEM((256, 8 * ROWS), f32),
+            pltpu.VMEM((128, 8 * ROWS), bf16),
+            pltpu.VMEM((128, 8 * ROWS), bf16),
+            pltpu.VMEM((4, 8 * ROWS), f32),
+            pltpu.VMEM((2, 256), f32),
             *[pltpu.VMEM(s, bf16) for s in scatter_shapes()],
             dma((n, 3, 6)),
             dma((n, 3, 6)),
@@ -611,47 +904,13 @@
             dma((8,)),
             dma((12,)),
             dma((12,)),
+            dma((10,)),
             dma((6,)),
+            dma((n, 4)),
             dma((6,)),
         ],
         compiler_params=pltpu.CompilerParams(collective_id=2, has_side_effects=True, vmem_limit_bytes=VMEM_MOST),
-    )(attn_own, attn_other, ffn, gains)
-
-
-def pair_kernel(reduce, src, out, stage, land, send_sem, recv_sem, local_sem):
-    at = coords()
-    mirror = device(at, t=1 - at["t"])
-    mine = pl.ds(pl.multiple_of(at["t"] * 128, 128), 128)
-    theirs = pl.ds(pl.multiple_of((1 - at["t"]) * 128, 128), 128)
-    if reduce:
-        stage[...] = src[theirs, :].astype(bf16)
-        enter([mirror])
-        copy = remote(stage, land, send_sem, recv_sem, mirror)
-        copy.start()
-        copy.wait()
-        out[...] = src[mine, :] + land[...].astype(f32)
-    else:
-        enter([mirror])
-        copy = remote(src, land, send_sem, recv_sem, mirror)
-        copy.start()
-        out[mine, :] = src[...]
-        copy.wait()
-        out[theirs, :] = land[...]
-
-
-def pair_call(value, reduce, number):
-    rows, width = value.shape
-    dma = pltpu.SemaphoreType.DMA
-    out = (rows // 2, width) if reduce else (rows * 2, width)
-    return pl.pallas_call(
-        functools.partial(pair_kernel, reduce),
-        name="pair_sum" if reduce else "pair_gather",
-        out_shape=jax.ShapeDtypeStruct(out, f32 if reduce else bf16),
-        in_specs=[VMEM_SPEC],
-        out_specs=VMEM_SPEC,
-        scratch_shapes=[pltpu.VMEM((128, width), bf16), pltpu.VMEM((128, width), bf16), dma, dma, dma],
-        compiler_params=pltpu.CompilerParams(collective_id=number, has_side_effects=True),
-    )(value)
+    )(*operands)
 
 
 def ffn_kernel(
@@ -668,7 +927,7 @@
     for j in range(pairs):
         for n in range(3):
             lo = n * 14 + 2 * j
-            copy = pltpu.make_async_copy(buf.at[6 + lo : 8 + lo], w.at[lo : lo + 2], w_sem.at[j, n])
+            copy = pltpu.make_async_copy(buf.at[place(lo) : place(lo) + 2], w.at[lo : lo + 2], w_sem.at[j, n])
             copy.start()
 
     def rows(c, t, n=1):
@@ -828,116 +1087,24 @@
     gain_post_ffn,
     cotangent,
 ):
-    my_dp, my_t = lax.axis_index("dp"), lax.axis_index("tensor")
-    core = lax.rem(my_dp, 2)
+    my_dp = lax.axis_index("dp")
     packed = jnp.concatenate(
         [gain_pre_attn, gain_post_attn, gain_pre_ffn, gain_post_ffn, gain_query, gain_key]
     ).astype(f32)
     packed = jnp.broadcast_to(jnp.pad(packed, (0, 48))[None], (8, 128))
-    buf, other, all_gains, both_tokens = gather_all(
-        (w_query, w_key, w_value, w_out, w_gate, w_up, w_down), packed, tokens
+    width = tokens.shape[1]
+    segment_row = segment_ids[0]
+    cos, sin = rope_tables(positions_of(segment_row), 256)
+    allowed = build_allowed(segment_row).astype(f32)
+    (
+        buf, other, attn_in, q_raw, k_raw, value, q_rot, k_rot, soft, context, attn_raw, residual, ffn_in, gain_d, gain_h,
+    ) = gather_all((w_query, w_key, w_value, w_out, w_gate, w_up, w_down), packed, tokens, cos, sin, allowed)
+    output, d_ffn, gpp, ffn_grads = ffn_all(ffn_in, residual, cotangent, gain_d[3:4], buf.reshape(48, width, 128))
+    sums = scatter_all(
+        ffn_grads.reshape(42, 2, 4, ROWS, 128), buf, other, attn_in, q_raw, k_raw, value, q_rot, k_rot, soft, context,
+        attn_raw, residual, d_ffn, cotangent, tokens, gain_d, gain_h, gpp, cos, sin,
     )
-    width = tokens.shape[1]
-    buf = buf.reshape(48, width, 128)
-    mine, other = buf[:6], other.reshape(6, width, 128)
-
-    def matrix(blocks):
-        return jnp.moveaxis(blocks, 0, 1).reshape(width, -1)
-
-    first = jnp.where(core == 0, mine, other)
-    second = jnp.where(core == 0, other, mine)
-    query_mat, key_mat = matrix(first[:4]), matrix(first[4:])
-    value_mat, out_mat = matrix(second[:2]), matrix(second[2:])
-    all_gains = all_gains.reshape(64, 128)
-    gain_pa, gain_po, gain_pf, gain_pp = [all_gains[:, 18 * n : 18 * n + 18].reshape(width) for n in range(4)]
-    gain_q, gain_k = [all_gains[:, 72 + 4 * n : 76 + 4 * n].reshape(256) for n in range(2)]
-    head_size = key_mat.shape[1]
-    heads_local = query_mat.shape[1] // head_size
-    resid_in = tokens.astype(f32)
-    r_one = lax.rsqrt(jnp.mean(resid_in * resid_in, axis=-1, keepdims=True) + eps)
-    attn_in = rms_apply(both_tokens.reshape(-1, width).astype(f32), gain_pa)[0].astype(bf16)
-    row_count = attn_in.shape[0]
-    segment_row = segment_ids[0]
-    position = positions_of(segment_row)
-    allowed = build_allowed(segment_row)
-    query_raw = jnp.dot(attn_in, query_mat, preferred_element_type=f32).reshape(
-        row_count, heads_local, head_size
-    )
-    key_raw = jnp.dot(attn_in, key_mat, preferred_element_type=f32)
-    value_vec = jnp.dot(attn_in, value_mat, preferred_element_type=f32).astype(bf16)
-    query_norm, r_query = rms_apply(query_raw, gain_q)
-    key_norm, r_key = rms_apply(key_raw, gain_k)
-    cosine_table, sine_table = rope_tables(position, head_size)
-    query_rot = (
-        query_norm * cosine_table[:, None, :] + rotate_half(query_norm) * sine_table[:, None, :]
-    ).astype(bf16)
-    key_rot = (key_norm * cosine_table + rotate_half(key_norm) * sine_table).astype(bf16)
-    score_scale = head_size ** (-0.5)
-    scores = jnp.einsum("qhd,kd->hqk", query_rot, key_rot, preferred_element_type=f32) * score_scale
-    scores = jnp.where(allowed[None], scores, -jnp.inf)
-    row_max = jnp.max(scores, axis=-1, keepdims=True)
-    row_total = jnp.sum(jnp.exp(scores - row_max), axis=-1, keepdims=True)
-    log_total = row_max + jnp.log(row_total)
-    weights_full = jnp.where(allowed[None], jnp.exp(scores - log_total), 0.0)
-    probs = weights_full.astype(bf16)
-    context = (
-        jnp.einsum("hqk,kd->qhd", probs, value_vec, preferred_element_type=f32)
-        .astype(bf16)
-        .reshape(row_count, heads_local * head_size)
-    )
-    attn_part = jnp.einsum("te,de->td", context, out_mat, preferred_element_type=f32)
-    attn_raw = pair_call(attn_part, True, 4)
-    attn_normed, r_two = rms_apply(attn_raw, gain_po)
-    residual = resid_in + attn_normed
-    ffn_local, r_three = rms_apply(residual, gain_pf)
-    output, d_ffn_input, grad_gpp, ffn_grads = ffn_all(
-        ffn_local.astype(bf16), residual, cotangent, gain_pp[None], buf
-    )
-    grad_out = cotangent.astype(f32)
-    d_resid_norm, grad_gpf = rms_back(residual, r_three, gain_pf, d_ffn_input)
-    d_residual = grad_out + d_resid_norm
-    d_attn_local, grad_gpo = rms_back(attn_raw, r_two, gain_po, d_residual)
-    d_attn_raw = pair_call(d_attn_local.astype(bf16), False, 5)
-    d_context = jnp.dot(d_attn_raw, out_mat, preferred_element_type=f32).astype(bf16)
-    grad_out_mat = jnp.einsum("td,te->de", d_attn_raw, context, preferred_element_type=f32)
-    d_context = d_context.reshape(row_count, heads_local, head_size)
-    d_prob = jnp.einsum("qhd,kd->hqk", d_context, value_vec, preferred_element_type=f32)
-    delta = jnp.sum(weights_full * d_prob, axis=-1, keepdims=True)
-    d_score = (weights_full * (d_prob - delta) * score_scale).astype(bf16)
-    d_query_rot = jnp.einsum("hqk,kd->qhd", d_score, key_rot, preferred_element_type=f32)
-    d_query_norm = d_query_rot * cosine_table[:, None, :] - rotate_half(
-        d_query_rot * sine_table[:, None, :]
-    )
-    d_query, grad_gq = rms_back(query_raw, r_query, gain_q, d_query_norm)
-    d_query = d_query.astype(bf16).reshape(row_count, heads_local * head_size)
-    d_key_rot = jnp.einsum("hqk,qhd->kd", d_score, query_rot, preferred_element_type=f32)
-    d_key_norm = d_key_rot * cosine_table - rotate_half(d_key_rot * sine_table)
-    d_key, grad_gk = rms_back(key_raw, r_key, gain_k, d_key_norm)
-    d_key = d_key.astype(bf16)
-    d_value = jnp.einsum("hqk,qhd->kd", probs, d_context, preferred_element_type=f32).astype(bf16)
-    d_in_part = jnp.einsum("te,de->td", d_query, query_mat, preferred_element_type=f32)
-    d_in_part = d_in_part + jnp.einsum("te,de->td", d_key, key_mat, preferred_element_type=f32)
-    d_in_part = d_in_part + jnp.einsum("te,de->td", d_value, value_mat, preferred_element_type=f32)
-    d_attn_in = pair_call(d_in_part, True, 6)
-    grad_query = jnp.einsum("td,te->de", attn_in, d_query, preferred_element_type=f32)
-    grad_key = jnp.einsum("td,te->de", attn_in, d_key, preferred_element_type=f32)
-    grad_value = jnp.einsum("td,te->de", attn_in, d_value, preferred_element_type=f32)
-    d_input_norm, grad_gpa = rms_back(resid_in, r_one, gain_pa, d_attn_in)
-    grad_tokens = d_residual + d_input_norm
-
-    def blocks(grad):
-        return jnp.moveaxis(grad.astype(bf16).reshape(width, -1, 128), 1, 0)
-
-    one = jnp.concatenate([blocks(grad_query), blocks(grad_key)])
-    two = jnp.concatenate([blocks(grad_value), blocks(grad_out_mat)])
-    shape = (6, 2, 4, ROWS, 128)
-    attn_own = jnp.where(core == 0, one, two).reshape(shape)
-    attn_other = jnp.where(core == 0, two, one).reshape(shape)
-    small = [g.reshape(64, 18) for g in (grad_gpa, grad_gpo, grad_gpf, grad_gpp)]
-    small += [g.reshape(64, 4) for g in (grad_gq, grad_gk)]
-    small = jnp.pad(jnp.concatenate(small, axis=1), ((0, 0), (0, 48))).reshape(2, 4, 8, 128)
-    sums = scatter_all(attn_own, attn_other, ffn_grads.reshape(42, 2, 4, ROWS, 128), small)
-    s_query, s_key, s_value, s_out, s_gate, s_up, s_down, s_gains = sums
+    s_query, s_key, s_value, s_out, s_gate, s_up, s_down, s_gains, grad_tokens = sums
     s_gains = lax.dynamic_index_in_dim(s_gains, lax.rem(my_dp, 8), 0, keepdims=False)
     s_pa, s_po, s_pf, s_pp = [s_gains[18 * n : 18 * n + 18] for n in range(4)]
     return (

time: 402 us -> 301 us (0.75)
  Pallas kernels: 308 us -> 268 us
  other arithmetic: 27.5 us -> 4.19 us
  local copies, waits for them, and re-layouts: 41.9 us -> 22.6 us
  matrix products: 16.5 us -> 0 us
    pallas_call x5 -> x2, Pallas kernels: 227 us -> 189 us  [the longest x1 94.9 us: scatter_all(): pl.pallas_call(scatter_kernel, name='attend_back_and_scatter', out_shape=...]
    dot_general x18 -> x0, matrix products: 16.5 us -> none  [the longest x1 1.74 us: local(): jnp.einsum('hqk,kd->qhd', d_score, key_rot, preferred_element_type=f32)]
    reduce_sum x9 -> x0, other arithmetic: 9.69 us -> none  [the longest x5 5.77 us: rms_back(): jnp.sum(grad_out * values * inverse, axis=tuple(range(values.ndim - 1)))]
    reshape x10 -> x0, local copies, waits for them, and re-layouts: 7.94 us -> none  [the longest x4 5.98 us: blocks(): return jnp.moveaxis(grad.astype(bf16).reshape(width, -1, 128), 1, 0)]
    transpose x6 -> x0, local copies, waits for them, and re-layouts: 6.74 us -> none  [matrix(): return jnp.moveaxis(blocks, 0, 1).reshape(width, -1)]
    select_n x2 -> x0, other arithmetic: 4.96 us -> none  [the longest x1 3.14 us: local(): attn_other = jnp.where(core == 0, two, one).reshape(shape)]
    unnamed x112 -> x11, local copies, waits for them, and re-layouts: 17.2 us -> 13.3 us
where the time goes in v2:
time: 301 us; the launch traced here: 296 us
  Pallas kernels  268 us (89%)
  local copies, waits for them, and re-layouts  22.6 us (8%)
  other arithmetic  4.19 us (1%)
    pallas_call x1, Pallas kernels, scatter_all(): pl.pallas_call(scatter_kernel, name='attend_back_and_scatter', out_shape=...  94.9 us
    pallas_call x1, Pallas kernels, gather_all(): pl.pallas_call(gather_kernel, name='gather_and_attend', out_shape=(shape(...  94.3 us
    pallas_call x1, Pallas kernels, ffn_all(): pl.pallas_call(ffn_kernel, name='ffn_layer', out_shape=(jax.ShapeDtypeStr...  78.8 us
    unnamed x11, local copies, waits for them, and re-layouts  13.3 us

profile of v2, /device:TPU:45, one launch (start us, length us, event | category | flops | bytes accessed | tf_op | source)
XLA Modules:
  0.0 296.2 jit_solution(3190142437933993999)
XLA Ops:
  0.6 4.1 %concatenate.14 = bf16[80]{0:T(256)(128)(2,1)S(1)} concatenate(bf16[18]{0:T(256)(128)(2,1)} %param.24, bf16[18]{0:T(256)(128)(2,1)} %param.25, bf16[18]{0:T(256)(128)(2,1)} %param.29, bf16[18]{0:T(256)(128)(2,1)} %param.30, bf16[4]{0:T(256)(128)(2,1)} %param.22, bf16[4]{0:T(256)(128)(2,1)} %param.23), dimensions={0} | concatenate | bytes 320 | tf_op jit(solution)/shard_map/concatenate | solution.py:1091
  4.8 0.6 broadcast_in_dim.6.gains_ref
  5.4 1.2 slice.56
  7.2 0.8 compare_select_fusion
  8.0 0.3 reduce-window.9
  8.3 0.1 slice.59
  8.4 0.1 slice_reduce_fusion
  8.6 0.1 fusion.2
  8.6 0.5 multiply_sine_fusion
  9.2 0.8 pad_maximum_fusion
  10.0 1.6 fusion.1.allowed_ref
  11.6 94.3 %gather_and_attend.1 = (bf16[4,12,2,4,144,128]{5,4,3,2,1,0:T(8,128)(2,1)}, bf16[3,2,2,4,144,128]{5,4,3,2,1,0:T(8,128)(2,1)}, bf16[256,1152]{1,0:T(8,128)(2,1)}, ...) custom-call(bf16[18,512]{1,0:T(8,128)(2,1)} %q_ref.1, ...), custom_call_target="tpu_custom_call" | custom-call | tf_op jit(solution)/shard_map/gather_and_attend/pallas_call | solution.py:496
  105.9 1.3 slice.61.gain
  107.2 78.8 %ffn_layer.1 = (bf16[128,1152]{1,0:T(8,128)(2,1)}, f32[128,1152]{1,0:T(8,128)}, f32[1,1152]{1,0:T(1,128)}, bf16[42,1152,128]{2,1,0:T(8,128)(2,1)}) custom-call(bf16[128,1152]{1,0:T(8,128)(2,1)} %get-tuple-element.43.x_in, f32[128,1152]{1,0:T(8,128)} %get-tuple-element.44.res.residual, bf16[128,1152]{1,0:T(8,128)(2,1)} %cot.3, f32[1,1152]{1,0:T(1,128)} %slice.61.gain, ...), custom_call_target="tpu_custom_call" | custom-call | tf_op jit(solution)/shard_map/ffn_layer/pallas_call | solution.py:1037
  186.0 0.0 copy-start
  186.1 94.9 %attend_back_and_scatter.1 = (f32[18,512]{1,0:T(8,128)}, f32[18,256]{1,0:T(8,128)}, f32[18,256]{1,0:T(8,128)}, f32[18,512]{1,0:T(8,128)}, f32[18,3456]{1,0:T(8,1...) custom-call(bf16[42,2,4,144,128]{4,3,2,1,0:T(8,128)(2,1)} %bitcast.28, ...), custom_call_target="tpu_custom_call" | custom-call | tf_op jit(solution)/shard_map/attend_back_and_scatter/pallas_call | solution.py:868
  281.0 0.7 constant_dynamic-slice_fusion
  281.7 0.6 slice_bitcast_fusion.4
  282.2 0.6 slice_bitcast_fusion
  282.8 0.0 copy-done
  282.8 0.7 copy.40
  283.6 1.9 copy.41
  285.5 1.4 copy.42
  286.9 1.3 copy.43
  288.2 1.3 copy.44
  289.6 1.4 copy.45
  291.0 1.7 copy.46
  292.7 1.7 copy.47
  294.4 1.7 copy.48
  (3 shorter events, 0.1 us)
Async XLA Ops:
  186.0 96.8 %copy-start = (bf16[128,1152]{1,0:T(8,128)(2,1)S(1)}, bf16[128,1152]{1,0:T(8,128)(2,1)}, u32[]{:S(2)}) copy-start(bf16[128,1152]{1,0:T(8,128)(2,1)} %get-tuple-element.96) | copy-start | bytes 884740

commit v3 on v2

--- a/solution.py
+++ b/solution.py
@@ -11,31 +11,6 @@
 eps = 1e-06
 gelu_scale = 0.7978845608028654
 gelu_cube = 0.044715
-
-
-def positions_of(segment_row):
-    token_index = jnp.arange(segment_row.shape[0], dtype=jnp.int32)
-    earlier = jnp.concatenate([segment_row[:1] - 1, segment_row[:-1]])
-    starts = lax.cummax(jnp.where(segment_row != earlier, token_index, 0), axis=0)
-    return token_index - starts
-
-
-def build_allowed(segment_row):
-    token_index = jnp.arange(segment_row.shape[0], dtype=jnp.int32)
-    same_seq = segment_row[:, None] == segment_row[None, :]
-    causal = token_index[None, :] <= token_index[:, None]
-    return same_seq & causal
-
-
-def rope_tables(position, width):
-    half_width = width // 2
-    frequency = jnp.exp(
-        jnp.arange(half_width, dtype=jnp.float32) * (-2.0 * math.log(10000.0) / width)
-    )
-    angles = position.astype(jnp.float32)[:, None] * frequency[None, :]
-    cosine_table = jnp.concatenate([jnp.cos(angles), jnp.cos(angles)], axis=1)
-    sine_table = jnp.concatenate([jnp.sin(angles), jnp.sin(angles)], axis=1)
-    return (cosine_table, sine_table)
 
 
 f32 = jnp.float32
@@ -184,6 +159,22 @@
     return events
 
 
+def write_tables(seg_ref, cos_ref, sin_ref, allowed_ref):
+    rows = seg_ref.shape[1]
+    across = jnp.broadcast_to(seg_ref[...].astype(f32), (rows, rows))
+    same = across == across.T
+    a = lax.broadcasted_iota(jnp.int32, (rows, rows), 0).astype(f32)
+    b = lax.broadcasted_iota(jnp.int32, (rows, rows), 1).astype(f32)
+    allowed_ref[...] = jnp.where(same & (b <= a), 1.0, 0.0)
+    begin = jnp.min(jnp.where(same, b, float(rows)), axis=1, keepdims=True)
+    position = a[:, :128] - begin
+    j = lax.broadcasted_iota(jnp.int32, (rows, 128), 1).astype(f32)
+    angles = position * jnp.exp(j * (-2.0 * math.log(10000.0) / 256))
+    for table, values in ((cos_ref, jnp.cos(angles)), (sin_ref, jnp.sin(angles))):
+        table[:, :128] = values
+        table[:, 128:] = values
+
+
 def normed(values, gain):
     inverse = lax.rsqrt(jnp.mean(values * values, axis=-1, keepdims=True) + eps)
     return values * inverse * (1.0 + gain), inverse
@@ -284,10 +275,10 @@
 
 
 def gather_kernel(
-    q_ref, k_ref, v_ref, o_ref, g_ref, u_ref, d_ref, gains_ref, tok_ref, cos_ref, sin_ref, allowed_ref,
-    buf, other, attn_in, q_raw, k_raw, value, q_rot, k_rot, soft, context, attn_raw, residual, ffn_in, gain_d, gain_h,
-    send, got, own32, own, ggot, gmine, gbuf, tok_out, w, part, pstage, pland,
-    a_send, a_recv, g_send, g_recv, s_sem, r_sem, e_sem, l_sem, w_sem,
+    q_ref, k_ref, v_ref, o_ref, g_ref, u_ref, d_ref, gains_ref, tok_ref, seg_ref,
+    buf, other, attn_in, q_raw, k_raw, value, q_rot, k_rot, soft, context, attn_raw, residual, ffn_full, gain_d, gain_h, cos_ref, sin_ref,
+    send, got, own32, own, ggot, gmine, gbuf, tok_out, w, part, pstage, pland, allowed_ref,
+    a_send, a_recv, g_send, g_recv, s_sem, r_sem, e_sem, l_sem, w_sem, x_sem,
 ):
     at = coords()
     refs = {"q": q_ref, "k": k_ref, "v": v_ref, "o": o_ref, "g": g_ref, "u": u_ref, "d": d_ref}
@@ -321,6 +312,7 @@
         first += [copy, small]
     here = pltpu.make_async_copy(send.at[me], got.at[mine], l_sem.at[0])
     here.start()
+    write_tables(seg_ref, cos_ref, sin_ref, allowed_ref)
     here.wait()
     for p in group:
         s = p["y"] * 2 + p["c"]
@@ -441,10 +433,26 @@
         attn_raw[...] = raw
         res = tok_ref[...].astype(f32) + normed(raw, gain_d[1:2, :])[0]
         residual[...] = res
-        ffn_in[...] = normed(res, gain_d[2:3, :])[0].astype(bf16)
-
-    pieces += [pair_start, pair_end]
-    for event in order_gather(CLASSES, ATTN_CLASSES, (0.0, 0.0, 3.0, 6.0, 9.0, 12.0, 15.0, 18.0, 20.0, 33.0)):
+        ffn_full[quarter(at["c"], at["t"]), :] = normed(res, gain_d[2:3, :])[0].astype(bf16)
+        for copy in spread[:2]:
+            copy.start()
+
+    def pass_on():
+        spread[0].wait_recv()
+        spread[2].start()
+
+    def quarter(c, t):
+        return pl.ds(pl.multiple_of((c * 2 + t) * 128, 128), 128)
+
+    mine_q = ffn_full.at[quarter(at["c"], at["t"]), :]
+    far_q = ffn_full.at[quarter(at["c"], 1 - at["t"]), :]
+    spread = [
+        remote(mine_q, mine_q, x_sem.at[0], x_sem.at[1], mirror),
+        remote(mine_q, mine_q, x_sem.at[2], x_sem.at[3], partner),
+        remote(far_q, far_q, x_sem.at[4], x_sem.at[5], partner),
+    ]
+    pieces += [pair_start, pair_end, pass_on]
+    for event in order_gather(CLASSES, ATTN_CLASSES, (0.0, 0.0, 3.0, 6.0, 9.0, 12.0, 15.0, 18.0, 20.0, 31.0, 42.0)):
         if len(event) == 1:
             pieces[event[0]]()
             continue
@@ -482,9 +490,12 @@
     for copy in pending:
         copy.wait_send()
     tok.wait_send()
-
-
-def gather_all(w, gains, tokens, cos, sin, allowed):
+    spread[0].wait_send()
+    spread[1].wait()
+    spread[2].wait()
+
+
+def gather_all(w, gains, tokens, segments):
     n = len(CLASSES)
     dma = pltpu.SemaphoreType.DMA
     half, width = tokens.shape
@@ -509,12 +520,14 @@
             shape(rows, 512, kind=bf16),
             shape(half, width),
             shape(half, width),
-            shape(half, width, kind=bf16),
+            shape(4 * half, width, kind=bf16),
             shape(4, width),
             shape(2, 256),
+            shape(rows, 256),
+            shape(rows, 256),
         ),
-        in_specs=[VMEM_SPEC] * 12,
-        out_specs=[ANY_SPEC] * 2 + [VMEM_SPEC] * 13,
+        in_specs=[VMEM_SPEC] * 10,
+        out_specs=[ANY_SPEC] * 2 + [VMEM_SPEC] * 15,
         scratch_shapes=[
             pltpu.VMEM((8, 12, SHARD, 128), bf16),
             pltpu.VMEM((8, 12, SHARD, 128), bf16),
@@ -528,6 +541,7 @@
             pltpu.VMEM((rows, width), f32),
             pltpu.VMEM((half, width), bf16),
             pltpu.VMEM((half, width), bf16),
+            pltpu.VMEM((rows, rows), f32),
             dma((8,)),
             dma((8,)),
             dma((12,)),
@@ -537,9 +551,10 @@
             dma((12,)),
             dma((3,)),
             dma((6,)),
+            dma((6,)),
         ],
         compiler_params=pltpu.CompilerParams(collective_id=1, has_side_effects=True, vmem_limit_bytes=VMEM_MOST),
-    )(*w, gains, tokens, cos, sin, allowed)
+    )(*w, gains, tokens, segments)
 
 
 def order_scatter(classes, late, pieces, begin, rate=46e3, hop=2.5):
@@ -615,10 +630,10 @@
 
 def scatter_kernel(
     ffn, buf, other, attn_in, q_raw, k_raw, value, q_rot, k_rot, soft, context, attn_raw, residual,
-    d_ffn, cot, tok, gain_d, gain_h, gpp, cos, sin,
-    q_out, k_out, v_out, o_out, g_out, u_out, d_out, gains_out, tok_out,
-    acc, pair, own32, send, got, gacc, grecv, ggot, kv, kvr, gfin, gfinal, gother,
-    w, ag, dfull, dctx, dq, dk, dv, part, pstage, pland, gsmall, gheads, *rest,
+    d_part, cot, tok, gain_d, gain_h, gpp, cos, sin,
+    got, kv_out, gains_out, tok_out,
+    acc, pair, own32, send, gacc, grecv, ggot, kv, kvr, gfin, gfinal, gother,
+    w, ag, dfull, dctx, dq, dk, dv, part, pstage, pland, gsmall, gheads, land_c, zstage, zland, *rest,
 ):
     lands = rest[:-10]
     s_sem, r_sem, a_send, a_recv, g_send, g_recv, e_sem, l_sem, f_sem, w_sem = rest[-10:]
@@ -640,12 +655,6 @@
             copy.start()
     near = pl.ds(pl.multiple_of(at["t"] * 128, 128), 128)
     far = pl.ds(pl.multiple_of((1 - at["t"]) * 128, 128), 128)
-    back, gsmall[2:3, :] = norm_back(residual[...], gain_d[2:3, :], d_ffn[...])
-    d_res = cot[...].astype(f32) + back
-    tok_out[...] = d_res
-    back, gsmall[1:2, :] = norm_back(attn_raw[...], gain_d[1:2, :], d_res)
-    dfull[near, :] = back.astype(bf16)
-    gsmall[3:4, :] = gpp[...]
     base = at["c"] * 6
     wloads = []
     for y in range(3):
@@ -665,7 +674,30 @@
         remote(ref, ref, s_sem.at[0, 0, 0], sem, partner).wait_recv()
 
     zo = device(at, z=1 - at["z"])
-    push(dfull.at[near, :], dfull.at[near, :], e_sem.at[6], e_sem.at[7], mirror)
+
+    def quarter(c, t, n=1):
+        return pl.ds(pl.multiple_of((c * 2 + t) * 128, 128), 128 * n)
+
+    over = remote(d_part.at[quarter(1 - at["c"], 0, 2), :], land_c, e_sem.at[10], e_sem.at[11], partner)
+    cross = remote(zstage, zland, e_sem.at[12], e_sem.at[13], mirror)
+    over.start()
+
+    def reduce_start():
+        over.wait()
+        zstage[...] = (d_part[quarter(at["c"], 1 - at["t"]), :] + land_c[far, :]).astype(bf16)
+        cross.start()
+
+    def reduce_end():
+        cross.wait()
+        d_ffn = d_part[quarter(at["c"], at["t"]), :] + land_c[near, :] + zland[...].astype(f32)
+        back, gsmall[2:3, :] = norm_back(residual[...], gain_d[2:3, :], d_ffn)
+        d_res = cot[...].astype(f32) + back
+        tok_out[...] = d_res
+        back, gsmall[1:2, :] = norm_back(attn_raw[...], gain_d[1:2, :], d_res)
+        dfull[near, :] = back.astype(bf16)
+        gsmall[3:4, :] = gpp[...]
+        push(dfull.at[near, :], dfull.at[near, :], e_sem.at[6], e_sem.at[7], mirror)
+
     swap = remote(ag.at[pl.ds(6 - base, 6)], pair, e_sem.at[0], e_sem.at[1], partner)
     pair_copy = remote(pstage, pland, e_sem.at[8], e_sem.at[9], mirror)
 
@@ -743,8 +775,8 @@
             xx = ahead(at, "x", n)
             push(gacc.at[at["z"], xx], grecv.at[4 + n], g_send.at[8 + n], g_recv.at[8 + n], device(at, x=xx))
 
-    pieces = [contexts, heads, weight_grads, out_grads, inputs, merge, finish, small_x]
-    times = (11.0, 14.0, 18.0, 21.0, 23.0, 26.0, 37.0, 41.0)
+    pieces = [reduce_start, reduce_end, contexts, heads, weight_grads, out_grads, inputs, merge, finish, small_x]
+    times = (3.0, 13.0, 25.0, 28.0, 32.0, 35.0, 37.0, 40.0, 50.0, 54.0)
     slots, position = {}, 0
     for k, (i0, i1, order) in enumerate(CLASSES):
         for ph in range(3):
@@ -752,7 +784,7 @@
             slots[k, ph] = lands[position : position + count]
             position += count
 
-    for event in order_scatter(CLASSES, ATTN_CLASSES, times, 26.1):
+    for event in order_scatter(CLASSES, ATTN_CLASSES, times, 40.1):
         if len(event) == 1:
             pieces[event[0]]()
             continue
@@ -833,49 +865,71 @@
     for s in range(1, 8):
         total = total + ggot[s]
     gfinal[...] = total
-    outs = {"q": q_out, "o": o_out, "g": g_out, "u": u_out, "d": d_out}
-    later = []
     for k, blocks in enumerate(block_sources()):
         for pos, source in enumerate(blocks):
-            if source is None:
-                continue
-            y, i = divmod(pos, 12)
-            name, j = source
-            if name in "kv":
-                j += 2 if name == "v" else 0
+            if source is not None and source[0] in "kv":
+                y, i = divmod(pos, 12)
+                j = source[1] + (2 if source[0] == "v" else 0)
                 kv[:, j * 128 : (j + 1) * 128] = got[k * 4 + y, i].astype(f32)
-            else:
-                later.append((name, j, k * 4 + y, i))
     push(kv, kvr, e_sem.at[2], e_sem.at[3], mirror)
     push(gfinal, gother, e_sem.at[4], e_sem.at[5], mirror)
-    for name, j, s, i in later:
-        outs[name][:, j * 128 : (j + 1) * 128] = got[s, i].astype(f32)
     await_ref(kvr, e_sem.at[3])
     await_ref(gother, e_sem.at[5])
-    k_out[...] = kv[:, 0:256] + kvr[:, 0:256]
-    v_out[...] = kv[:, 256:512] + kvr[:, 256:512]
+    kv_out[...] = kv[...] + kvr[...]
     gains_out[...] = gfinal[...] + gother[...]
     for copy in pending:
         copy.wait_send()
 
 
+def result_kernel(got, kv, gains, tok, res, q_out, k_out, v_out, o_out, g_out, u_out, d_out, tok_out, out, *gain_outs):
+    outs = {"q": q_out, "o": o_out, "g": g_out, "u": u_out, "d": d_out}
+    for k, blocks in enumerate(block_sources()):
+        for pos, source in enumerate(blocks):
+            if source is not None and source[0] not in "kv":
+                y, i = divmod(pos, 12)
+                name, j = source
+                outs[name][:, j * 128 : (j + 1) * 128] = got[k * 4 + y, i].astype(f32)
+    k_out[...] = kv[:, 0:256]
+    v_out[...] = kv[:, 256:512]
+    tok_out[...] = tok[...]
+    out[...] = res[...]
+    row = lax.broadcasted_iota(jnp.int32, (8, 128), 0)
+    line = jnp.sum(jnp.where(row == lax.rem(lax.axis_index("dp"), 8), gains[...], 0.0), axis=0, keepdims=True)
+    for n, ref in enumerate(gain_outs):
+        size = ref.shape[1]
+        lo = SHARD * n if n < 4 else 4 * SHARD + 4 * (n - 4)
+        ref[...] = line[:, lo : lo + size]
+
+
+def results(got, kv, gains, tok, res):
+    widths = (512, 256, 256, 512, 3456, 3456, 3456)
+    out = [jax.ShapeDtypeStruct((SHARD, w), f32) for w in widths]
+    out += [jax.ShapeDtypeStruct(tok.shape, f32), jax.ShapeDtypeStruct(res.shape, bf16)]
+    out += [jax.ShapeDtypeStruct((1, n), f32) for n in (SHARD, SHARD, SHARD, SHARD, 4, 4)]
+    return pl.pallas_call(
+        result_kernel,
+        name="assemble",
+        out_shape=tuple(out),
+        in_specs=[VMEM_SPEC] * 5,
+        out_specs=[VMEM_SPEC] * len(out),
+    )(got, kv, gains, tok, res)
+
+
 def scatter_all(*operands):
     n = len(CLASSES)
     dma = pltpu.SemaphoreType.DMA
-    widths = (512, 256, 256, 512, 3456, 3456, 3456)
-    out = [jax.ShapeDtypeStruct((SHARD, w), f32) for w in widths]
+    out = [jax.ShapeDtypeStruct((8, 12, SHARD, 128), bf16), jax.ShapeDtypeStruct((SHARD, 512), f32)]
     out += [jax.ShapeDtypeStruct((8, 128), f32), jax.ShapeDtypeStruct((128, 8 * ROWS), f32)]
     return pl.pallas_call(
         scatter_kernel,
         name="attend_back_and_scatter",
         out_shape=tuple(out),
         in_specs=[ANY_SPEC] * 3 + [VMEM_SPEC] * 18,
-        out_specs=[VMEM_SPEC] * 9,
+        out_specs=[VMEM_SPEC] * 4,
         scratch_shapes=[
             pltpu.VMEM((4, 12, 2, 4, ROWS, 128), bf16),
             pltpu.VMEM((6, 2, 4, ROWS, 128), bf16),
             pltpu.VMEM((ROWS, 128), f32),
-            pltpu.VMEM((8, 12, SHARD, 128), bf16),
             pltpu.VMEM((8, 12, SHARD, 128), bf16),
             pltpu.VMEM((2, 4, 8, 128), f32),
             pltpu.VMEM((8, 8, 128), f32),
@@ -897,6 +951,9 @@
             pltpu.VMEM((128, 8 * ROWS), bf16),
             pltpu.VMEM((4, 8 * ROWS), f32),
             pltpu.VMEM((2, 256), f32),
+            pltpu.VMEM((256, 8 * ROWS), f32),
+            pltpu.VMEM((128, 8 * ROWS), bf16),
+            pltpu.VMEM((128, 8 * ROWS), bf16),
             *[pltpu.VMEM(s, bf16) for s in scatter_shapes()],
             dma((n, 3, 6)),
             dma((n, 3, 6)),
@@ -904,7 +961,7 @@
             dma((8,)),
             dma((12,)),
             dma((12,)),
-            dma((10,)),
+            dma((14,)),
             dma((6,)),
             dma((n, 4)),
             dma((6,)),
@@ -914,9 +971,9 @@
 
 
 def ffn_kernel(
-    x_in, res, cot, gain, buf,
-    out, d_in, gpp, grads,
-    w, dw, xs, ds, xt, dt, gates, ups, part, land_a, land_b, zstage, zland_a, zland_b,
+    xs, res, cot, gain, buf,
+    out, part, gpp, grads,
+    w, dw, ds, xt, dt, gates, ups, land_a, zstage, zland_a,
     w_sem, dw_sem, s_sem, r_sem,
 ):
     at = coords()
@@ -933,7 +990,6 @@
     def rows(c, t, n=1):
         return pl.ds(pl.multiple_of((c * 2 + t) * 128, 128), 128 * n)
 
-    enter([mirror, partner])
     c, t = at["c"], at["t"]
 
     def gather(e, full):
@@ -965,8 +1021,6 @@
         b.wait()
         return kept + zland[...].astype(f32)
 
-    xs[rows(c, t), :] = x_in[...]
-    gather(0, xs)
     part[...] = jnp.zeros_like(part)
 
     def weights(j, n):
@@ -988,6 +1042,7 @@
         hidden = (act * up).astype(bf16)
         part[...] += rows_dot(hidden, weights(j, 2))
 
+    enter([mirror, partner])
     raw = reduce(1, land_a, zland_a)
     width = raw.shape[1]
     inverse = lax.rsqrt(jnp.sum(raw * raw, axis=-1, keepdims=True) * (1.0 / width) + eps)
@@ -1024,22 +1079,21 @@
             dw[lo + 1] = grad[:, 128:]
             pltpu.make_async_copy(dw.at[pl.ds(lo, 2)], grads.at[pl.ds(lo, 2)], dw_sem.at[j, n]).start()
 
-    d_in[...] = reduce(3, land_b, zland_b)
     for j in range(pairs):
         for n in range(3):
             lo = n * 14 + 2 * j
             pltpu.make_async_copy(dw.at[lo : lo + 2], grads.at[lo : lo + 2], dw_sem.at[j, n]).wait()
 
 
-def ffn_all(x_in, res, cot, gain, buf):
+def ffn_all(xs, res, cot, gain, buf):
     dma = pltpu.SemaphoreType.DMA
-    tokens, width = x_in.shape
+    tokens, width = res.shape
     return pl.pallas_call(
         ffn_kernel,
         name="ffn_layer",
         out_shape=(
             jax.ShapeDtypeStruct((tokens, width), bf16),
-            jax.ShapeDtypeStruct((tokens, width), f32),
+            jax.ShapeDtypeStruct((4 * tokens, width), f32),
             jax.ShapeDtypeStruct((1, width), f32),
             jax.ShapeDtypeStruct((42, width, 128), bf16),
         ),
@@ -1049,15 +1103,11 @@
             pltpu.VMEM((42, width, 128), bf16),
             pltpu.VMEM((42, width, 128), bf16),
             pltpu.VMEM((512, width), bf16),
-            pltpu.VMEM((512, width), bf16),
             pltpu.VMEM((width, 512), bf16),
             pltpu.VMEM((width, 512), bf16),
             pltpu.VMEM((512, 1792), f32),
             pltpu.VMEM((512, 1792), f32),
-            pltpu.VMEM((512, width), f32),
             pltpu.VMEM((256, width), f32),
-            pltpu.VMEM((256, width), f32),
-            pltpu.VMEM((128, width), bf16),
             pltpu.VMEM((128, width), bf16),
             pltpu.VMEM((128, width), bf16),
             dma((7, 3)),
@@ -1066,7 +1116,7 @@
             dma((4, 3)),
         ],
         compiler_params=pltpu.CompilerParams(collective_id=3, has_side_effects=True, vmem_limit_bytes=VMEM_MOST),
-    )(x_in, res, cot, gain, buf)
+    )(xs, res, cot, gain, buf)
 
 
 def local(
@@ -1087,28 +1137,27 @@
     gain_post_ffn,
     cotangent,
 ):
-    my_dp = lax.axis_index("dp")
-    packed = jnp.concatenate(
-        [gain_pre_attn, gain_post_attn, gain_pre_ffn, gain_post_ffn, gain_query, gain_key]
-    ).astype(f32)
-    packed = jnp.broadcast_to(jnp.pad(packed, (0, 48))[None], (8, 128))
+    gains = (gain_pre_attn, gain_post_attn, gain_pre_ffn, gain_post_ffn, gain_query, gain_key)
+    packed, lane = 0.0, 0
+    for gain in gains:
+        packed = packed + jnp.pad(gain.astype(f32), (lane, 128 - lane - gain.shape[0]))
+        lane += gain.shape[0]
+    packed = jnp.broadcast_to(packed[None], (8, 128))
     width = tokens.shape[1]
-    segment_row = segment_ids[0]
-    cos, sin = rope_tables(positions_of(segment_row), 256)
-    allowed = build_allowed(segment_row).astype(f32)
     (
-        buf, other, attn_in, q_raw, k_raw, value, q_rot, k_rot, soft, context, attn_raw, residual, ffn_in, gain_d, gain_h,
-    ) = gather_all((w_query, w_key, w_value, w_out, w_gate, w_up, w_down), packed, tokens, cos, sin, allowed)
-    output, d_ffn, gpp, ffn_grads = ffn_all(ffn_in, residual, cotangent, gain_d[3:4], buf.reshape(48, width, 128))
+        buf, other, attn_in, q_raw, k_raw, value, q_rot, k_rot, soft, context, attn_raw, residual, ffn_full,
+        gain_d, gain_h, cos, sin,
+    ) = gather_all((w_query, w_key, w_value, w_out, w_gate, w_up, w_down), packed, tokens, segment_ids)
+    output, d_part, gpp, ffn_grads = ffn_all(ffn_full, residual, cotangent, gain_d[3:4], buf.reshape(48, width, 128))
     sums = scatter_all(
         ffn_grads.reshape(42, 2, 4, ROWS, 128), buf, other, attn_in, q_raw, k_raw, value, q_rot, k_rot, soft, context,
-        attn_raw, residual, d_ffn, cotangent, tokens, gain_d, gain_h, gpp, cos, sin,
+        attn_raw, residual, d_part, cotangent, tokens, gain_d, gain_h, gpp, cos, sin,
     )
-    s_query, s_key, s_value, s_out, s_gate, s_up, s_down, s_gains, grad_tokens = sums
-    s_gains = lax.dynamic_index_in_dim(s_gains, lax.rem(my_dp, 8), 0, keepdims=False)
-    s_pa, s_po, s_pf, s_pp = [s_gains[18 * n : 18 * n + 18] for n in range(4)]
+    sums = results(*sums, output)
+    s_query, s_key, s_value, s_out, s_gate, s_up, s_down, grad_tokens, output = sums[:9]
+    s_pa, s_po, s_pf, s_pp, s_gq, s_gk = [g.reshape(-1) for g in sums[9:]]
     return (
-        output, grad_tokens, s_query, s_key, s_value, s_out, s_gains[72:76], s_gains[76:80],
+        output, grad_tokens, s_query, s_key, s_value, s_out, s_gq, s_gk,
         s_pa, s_po, s_gate, s_up, s_down, s_pf, s_pp,
     )
 

time: 301 us -> 277 us (0.920)
  local copies, waits for them, and re-layouts: 22.6 us -> 1.92 us
  other arithmetic: 4.19 us -> 0.82 us
    pallas_call x1, Pallas kernels: 78.8 us -> 60.2 us  [ffn_all(): pl.pallas_call(ffn_kernel, name='ffn_layer', out_shape=(jax.ShapeDtypeStr...]
    unnamed x11 -> x0, local copies, waits for them, and re-layouts: 13.3 us -> none
    pallas_call x1, Pallas kernels: 94.9 us -> 105 us  [scatter_all(): pl.pallas_call(scatter_kernel, name='attend_back_and_scatter', out_shape=...]
    pallas_call x1, Pallas kernels: 94.3 us -> 100 us  [gather_all(): pl.pallas_call(gather_kernel, name='gather_and_attend', out_shape=(shape(...]
    concatenate x1 -> x0, local copies, waits for them, and re-layouts: 4.1 us -> none  [local(): jnp.concatenate([gain_pre_attn, gain_post_attn, gain_pre_ffn, gain_post_f...]
where the time goes in v3:
time: 277 us; the launch traced here: 272 us
  Pallas kernels  269 us (97%)
    pallas_call x1, Pallas kernels, scatter_all(): pl.pallas_call(scatter_kernel, name='attend_back_and_scatter', out_shape=...  105 us
    pallas_call x1, Pallas kernels, gather_all(): pl.pallas_call(gather_kernel, name='gather_and_attend', out_shape=(shape(...  100 us
    pallas_call x1, Pallas kernels, ffn_all(): pl.pallas_call(ffn_kernel, name='ffn_layer', out_shape=(jax.ShapeDtypeStr...  60.2 us

profile of v3, /device:TPU:45, one launch (start us, length us, event | category | flops | bytes accessed | tf_op | source)
XLA Modules:
  0.0 272.1 jit_solution(2121546317929732304)
XLA Ops:
  0.6 0.8 convert_add_fusion
  1.5 0.6 broadcast_in_dim.2.gains_ref
  2.1 100.5 %gather_and_attend.1 = (bf16[4,12,2,4,144,128]{5,4,3,2,1,0:T(8,128)(2,1)}, bf16[3,2,2,4,144,128]{5,4,3,2,1,0:T(8,128)(2,1)}, bf16[256,1152]{1,0:T(8,128)(2,1)}, ...) custom-call(bf16[18,512]{1,0:T(8,128)(2,1)} %q_ref.1, ...), custom_call_target="tpu_custom_call" | custom-call | tf_op jit(solution)/shard_map/gather_and_attend/pallas_call | solution.py:507
  102.5 1.3 slice.3.gain
  103.8 60.2 %ffn_layer.1 = (bf16[128,1152]{1,0:T(8,128)(2,1)}, f32[512,1152]{1,0:T(8,128)}, f32[1,1152]{1,0:T(1,128)}, bf16[42,1152,128]{2,1,0:T(8,128)(2,1)}) custom-call(bf16[512,1152]{1,0:T(8,128)(2,1)} %get-tuple-element.55.xs, f32[128,1152]{1,0:T(8,128)} %get-tuple-element.56.res.residual, bf16[128,1152]{1,0:T(8,128)(2,1)} %cot.3, f32[1,1152]{1,0:T(1,128)} %slice.3.gain, ...), custom_call_target="tpu_custom_call" | custom-call | tf_op jit(solution)/shard_map/ffn_layer/pallas_call | solution.py:1091
  164.1 105.1 %attend_back_and_scatter.1 = (bf16[8,12,18,128]{3,2,1,0:T(8,128)(2,1)}, f32[18,512]{1,0:T(8,128)}, f32[8,128]{1,0:T(8,128)}, f32[128,1152]{1,0:T(8,128)}) custom-call(bf16[42,2,4,144,128]{4,3,2,1,0:T(8,128)(2,1)} %bitcast.9, bf16[4,12,2,4,144,128]{5,4,3,2,1,0:T(8,128)(2,1)} %get-tuple-element.58.buf, ...), custom_call_target="tpu_custom_call" | custom-call | tf_op jit(solution)/shard_map/attend_back_and_scatter/pallas_call | solution.py:923
  269.2 2.7 assemble.1
